TPU v7x, 32 devices: a whole 2x2x4 slice. The times are simulated.
32 devices in a mesh: lat: 4 (over z), lon: 8 (over y, x, core).
Axes of the slice: x: 2, y: 2, z: 4, core: 2. Of those that a mesh axis runs over, the one named last changes fastest.
Arguments:
- adjoint_in: float32 [2, 10, 512, 2048], P(None, None, 'lat', 'lon'), may hold values from -6 to 6
- east_flow: float32 [10, 512, 2048], P(None, 'lat', 'lon'), may hold values from -0.2 to 0.2
- north_flow: float32 [10, 512, 2048], P(None, 'lat', 'lon'), may hold values from -0.2 to 0.2
- diffusivity: float32 [2, 10], replicated, may hold values from 0.01 to 0.05
- land_mask: int32 [10, 512, 2048], P(None, 'lat', 'lon'), may hold values 0 or 1
- forcing: bfloat16 [32, 64, 2, 10, 128], P(('lat', 'lon')), may hold values from -6 to 6
- obs_tile: int32 [32, 64], P(('lat', 'lon')), may hold values from 0 to 31, as said below
- obs_block: int32 [32, 64], P(('lat', 'lon')), may hold values from 0 to 255
- obs_live: int32 [32], P(('lat', 'lon')), may hold values from 48 to 64, as said below
Outputs:
- adjoint_out: float32 [2, 10, 512, 2048], P(None, None, 'lat', 'lon')
Inputs may be any that keep to these rules, and one draw needn't show every extreme that they name: `obs_tile`: among the live records of one holder no tile is named more than 4 times. Records at positions obs_live[h] and beyond of holder h are not live.
All inputs are finite; a program needn't handle non-finite values. No bound on the sum of `land_mask` on one device may be relied on, other than what follows from the above.
Results may differ from a plain program's by a relative error of at most 0.0017.
Values may be sent and summed in bfloat16 or wider, within the bound.
No kernel may reach another device: no remote copies, remote signals or barrier semaphores. Data moves between devices by JAX's collectives and lax.ppermute only.
A program may use at most 128 MiB of HBM per device.

v0:
```python
import functools

import jax
import jax.numpy as jnp
from jax import lax
from jax.experimental import pallas as pl
from jax.experimental.pallas import tpu as pltpu
from jax.sharding import PartitionSpec as P

STEPS = 3
LANES = 128
F32 = jnp.float32
BF16 = jnp.bfloat16
HBM = pl.BlockSpec(memory_space=pltpu.HBM)
VMEM = pl.BlockSpec(memory_space=pltpu.VMEM)
SMEM = pl.BlockSpec(memory_space=pltpu.SMEM)


def iota(shape, dim):
    return lax.broadcasted_iota(jnp.int32, shape, dim)


def fiota(shape, dim):
    return iota(shape, dim).astype(F32)


def west_lane(shape):
    lane = fiota(shape, 1)
    return lane - 6.0 * jnp.floor((lane + 0.5) / 6.0) < 3.0


def one_hot(rows, code):
    shape = (rows, code.shape[1])
    return jnp.where(fiota(shape, 0) == code, 1.0, 0.0).astype(BF16)


def dot(a, b):
    return jnp.dot(a, b, preferred_element_type=F32)


def pack_body(
    n_lon, live_ref, tile_in, block_in, forcing_in, out_hbm,
    tile_ref, block_ref, forcing_ref, out_ref, wide, sems, out_sems,
):
    records, levels = forcing_ref.shape[1], forcing_ref.shape[2]
    count = 2 * levels
    devices = out_ref.shape[0]
    moves = [
        pltpu.make_async_copy(source, dest, sems.at[i])
        for i, (source, dest) in enumerate(
            (
                (tile_in, tile_ref),
                (block_in, block_ref),
                (forcing_in, forcing_ref),
            )
        )
    ]
    for move in moves:
        move.start()
    for move in moves[:2]:
        move.wait()
    tile = tile_ref[...].astype(F32)
    block = block_ref[...].astype(F32)
    square = (records, records)
    low, high = iota(square, 0), iota(square, 1)
    tile_col = jnp.sum(jnp.where(low == high, tile, 0.0), axis=1, keepdims=True)
    block_col = jnp.sum(jnp.where(low == high, block, 0.0), axis=1, keepdims=True)
    earlier = jnp.where((tile_col == tile) & (low < high), 1.0, 0.0)
    rank = jnp.sum(earlier, axis=0, keepdims=True)
    live = iota((1, records), 1) < live_ref[0]
    band = jnp.floor((tile + 0.5) / n_lon) * n_lon
    column = tile - band
    east = band + jnp.where(column == n_lon - 1, 0.0, column + 1.0)
    west = band + jnp.where(column == 0.0, n_lon - 1.0, column - 1.0)
    half = block - 2.0 * jnp.floor(block * 0.5)
    code = jnp.where(live, tile * 8.0 + rank, -8.0)
    to_east = jnp.where(live & (half == 1.0), east * 8.0 + rank, -8.0)
    to_west = jnp.where(live & (half == 0.0), west * 8.0 + rank, -8.0)
    moves[2].wait()

    def widen(r, carry):
        for level in range(levels):
            wide[pl.ds(r * count + 2 * level, 2), :] = forcing_ref[0, r, level].astype(F32)
        return carry

    lax.fori_loop(0, records, widen, 0, unroll=4)
    sent = []

    def send(q, values):
        out_ref[:, q] = values.astype(BF16).reshape(devices, 8, LANES)
        copy = pltpu.make_async_copy(out_ref.at[:, q], out_hbm.at[:, q], out_sems.at[q])
        copy.start()
        sent.append(copy)

    first, second = one_hot(devices * 8, code), one_hot(devices * 8, code + 4.0)
    lane = iota((records, LANES), 1)
    edges = jnp.zeros((records, LANES), F32)
    pair = []
    for place in range(count):
        level, t = divmod(place, 2)
        k = t * levels + level
        values = wide[pl.ds(place, records, stride=count), :]
        turned = pltpu.roll(values, (6 * k + 3) % LANES, 1)
        edges = jnp.where((lane >= 6 * k) & (lane < 6 * k + 6), turned, edges)
        pair.append(values.astype(BF16))
        if t == 1:
            packed = dot(first, pair[0]) + dot(second, pair[1])
            send(level, packed)
            pair = []
    row_col = jnp.floor(block_col * 0.5) + 1.0
    mine = west_lane((records, LANES))
    data = lane < 6 * count
    from_west = jnp.where(data, jnp.where(mine, edges, 0.0), jnp.where(lane == 121, row_col, 0.0))
    from_east = jnp.where(data, jnp.where(mine, 0.0, edges), jnp.where(lane == 122, row_col, 0.0))
    header = jnp.where(lane == 120, block_col + 1.0, 0.0)
    last = (
        dot(first, header.astype(BF16))
        + dot(one_hot(devices * 8, to_east), from_west.astype(BF16))
        + dot(one_hot(devices * 8, to_west), from_east.astype(BF16))
    )
    send(count // 2, last)
    for copy in sent:
        copy.wait()


def pack_records(forcing, tile, block, live, devices, n_lon):
    records, levels, width = forcing.shape[1], forcing.shape[2], forcing.shape[4]
    out = (devices, levels + 1, 8, width)
    return pl.pallas_call(
        functools.partial(pack_body, n_lon),
        name="pack_records",
        out_shape=pltpu.HBM(out, BF16),
        in_specs=[SMEM] + [HBM] * 3,
        out_specs=HBM,
        scratch_shapes=[
            pltpu.VMEM(tile.shape, jnp.int32),
            pltpu.VMEM(block.shape, jnp.int32),
            pltpu.VMEM(forcing.shape, BF16),
            pltpu.VMEM(out, BF16),
            pltpu.VMEM((records * levels * 2, width), F32),
            pltpu.SemaphoreType.DMA((3,)),
            pltpu.SemaphoreType.DMA((levels + 1,)),
        ],
        compiler_params=pltpu.CompilerParams(vmem_limit_bytes=24 << 20),
    )(live, *map(hbm, (tile, block, forcing)))


STRIPS = 3


def strip_of(k):
    return k // 7, 18 * lax.rem(k, 7) if not isinstance(k, int) else 18 * (k % 7)


def turn(values, shift):
    if isinstance(shift, int):
        return pltpu.roll(values, shift % LANES, 1)
    return pltpu.roll(values, lax.rem(shift + 4 * LANES, LANES), 1)


def hbm(x):
    return pltpu.with_memory_space_constraint(x, pltpu.HBM)


def between(lane, low, high):
    return (lane >= low) & (lane < high)


def columns_body(
    adj_hbm, ef_hbm, nf_hbm, mask_hbm, out_ref, ocean_ref, adj_ref, flow_ref, mask, held, sems
):
    levels, rows = mask.shape[0], mask.shape[1]

    def moves(level):
        pairs = [(mask_hbm.at[level], mask.at[level])]
        pairs += [(adj_hbm.at[t, level], adj_ref.at[t, level]) for t in range(2)]
        pairs += [
            (
                source.at[level, :, pl.ds(x * LANES, LANES)],
                flow_ref.at[level, f, x],
            )
            for f, source in enumerate((ef_hbm, nf_hbm))
            for x in range(2)
        ]
        return [
            pltpu.make_async_copy(source, dest, sems.at[i, level])
            for i, (source, dest) in enumerate(pairs)
        ]

    for level in range(levels):
        for copy in moves(level):
            copy.start()
    lane = iota((rows, LANES), 1)
    held[...] = jnp.zeros_like(held)

    def put(tile, place, first, second):
        ends = jnp.where(lane < 64, first, second)
        inside = between(lane, 6 * place, 6 * place + 6)
        held[tile] = jnp.where(inside, turn(ends, 6 * place + 3), held[tile])

    def one(level, carry):
        for copy in moves(level):
            copy.wait()
        for x in range(2):
            ocean_ref[level, x] = mask[level, :, x * LANES : (x + 1) * LANES].astype(F32)
        for t in range(2):
            put(0, t * levels + level, adj_ref[t, level, :, :LANES], adj_ref[t, level, :, LANES:])
        put(1, level, flow_ref[level, 0, 0], flow_ref[level, 0, 1])
        put(1, levels + level, flow_ref[level, 1, 0], flow_ref[level, 1, 1])
        put(2, level, ocean_ref[level, 0], ocean_ref[level, 1])
        return carry

    lax.fori_loop(0, levels, one, 0)
    for tile in range(3):
        out_ref[:, tile * LANES : (tile + 1) * LANES] = held[tile].astype(BF16)


def outer_columns(adj, ef, nf, mask):
    levels, rows, cells = ef.shape
    return pl.pallas_call(
        columns_body,
        name="outer_columns",
        out_shape=(
            jax.ShapeDtypeStruct((rows, 3 * LANES), BF16),
            jax.ShapeDtypeStruct((levels, 2, rows, LANES), F32),
        ),
        in_specs=[HBM] * 4,
        out_specs=(VMEM,) * 2,
        scratch_shapes=[
            pltpu.VMEM(adj.shape, F32),
            pltpu.VMEM((levels, 2, 2, rows, LANES), F32),
            pltpu.VMEM(mask.shape, jnp.int32),
            pltpu.VMEM((3, rows, LANES), F32),
            pltpu.SemaphoreType.DMA((7, levels)),
        ],
        compiler_params=pltpu.CompilerParams(vmem_limit_bytes=24 << 20),
    )(*map(hbm, (adj, ef, nf, mask)))


def own_body(ef_hbm, nf_hbm, ocean_ref, strips, spread_ref, flow_ref, sems):
    levels, rows = ocean_ref.shape[0], ocean_ref.shape[2]

    def moves(level):
        return [
            pltpu.make_async_copy(
                source.at[level, :, pl.ds(x * LANES, LANES)],
                flow_ref.at[level, f, x],
                sems.at[2 * f + x, level],
            )
            for f, source in enumerate((ef_hbm, nf_hbm))
            for x in range(2)
        ]

    for level in range(levels):
        for copy in moves(level):
            copy.start()
    square = (LANES, LANES)
    source, target = fiota(square, 0), fiota(square, 1)
    order = jnp.floor((target + 0.5) / 18.0)
    offset = target - 18.0 * order
    inner = jnp.where(offset < 3.0, offset, offset - 12.0)
    used = ((offset < 3.0) | (offset >= 15.0)) & (order < 7.0)
    for tile in range(STRIPS):
        k = order + 7.0 * tile
        level = jnp.where(k < levels, k, k - levels)
        live = used & (k < 2.0 * levels)
        for m, place in enumerate((k, level, level + levels)):
            hit = live & (source == 6.0 * place + inner)
            spread_ref[m, :, tile * LANES : (tile + 1) * LANES] = jnp.where(hit, 1.0, 0.0).astype(BF16)
    strips[...] = jnp.zeros_like(strips)
    lane = iota((rows, LANES), 1)

    def one(level, carry):
        for copy in moves(level):
            copy.wait()
        for f, ref in enumerate((flow_ref.at[level, 0], flow_ref.at[level, 1], ocean_ref.at[level])):
            own = jnp.where(lane < 9, turn(ref[0], 3), turn(ref[1], 15))
            for t in range(2):
                tile, first = strip_of(t * levels + level)
                keep = between(lane, first + 3, first + 15)
                strips[f, tile] = jnp.where(keep, turn(own, first), strips[f, tile])
        return carry

    lax.fori_loop(0, levels, one, 0)


def own_strips(ef, nf, ocean):
    levels, rows = ef.shape[0], ef.shape[1]
    return pl.pallas_call(
        own_body,
        name="own_strips",
        out_shape=(
            jax.ShapeDtypeStruct((3, STRIPS, rows, LANES), F32),
            jax.ShapeDtypeStruct((3, LANES, STRIPS * LANES), BF16),
        ),
        in_specs=[HBM, HBM, VMEM],
        out_specs=(VMEM, VMEM),
        scratch_shapes=[
            pltpu.VMEM((levels, 2, 2, rows, LANES), F32),
            pltpu.SemaphoreType.DMA((4, levels)),
        ],
        cost_estimate=pl.CostEstimate(flops=10**8, bytes_accessed=10**7, transcendentals=0),
        compiler_params=pltpu.CompilerParams(vmem_limit_bytes=24 << 20),
    )(hbm(ef), hbm(nf), ocean)


def edges_body(
    west, east, ef_hbm, nf_hbm, ocean_ref, own_ref, spread_ref,
    strips, adj, low_out, high_out, low, high, ends, sems,
):
    levels, rows = ocean_ref.shape[0], ocean_ref.shape[2]
    copies = [
        pltpu.make_async_copy(
            source.at[:, pl.ds(base, 8), :], ends.at[side, f], sems.at[side, f]
        )
        for side, base in ((0, 0), (1, rows - 8))
        for f, source in enumerate((ef_hbm, nf_hbm))
    ]
    for copy in copies:
        copy.start()
    low[...] = jnp.zeros_like(low)
    high[...] = jnp.zeros_like(high)

    def halo(tile, m):
        part = slice(tile * LANES, (tile + 1) * LANES)
        theirs, ours = west[:, part].astype(F32), east[:, part].astype(F32)
        merged = jnp.where(west_lane(theirs.shape), theirs, ours).astype(BF16)
        return dot(merged, spread_ref[m])

    halos = halo(0, 0)
    for tile in range(STRIPS):
        adj[tile] = halos[:, tile * LANES : (tile + 1) * LANES]
    for f, (source, m) in enumerate(((1, 1), (1, 2), (2, 1))):
        halos = halo(source, m)
        for tile in range(STRIPS):
            strips[f, tile] = own_ref[f, tile] + halos[:, tile * LANES : (tile + 1) * LANES]
    for copy in copies:
        copy.wait()
    for side, (out, first, near) in enumerate(((low, 0, 0), (high, rows - 3, 5))):
        strip_at = slice(first, first + 3)
        for f in range(3):
            here = slice(3 * f, 3 * f + 3)
            for level in range(levels):
                if f < 2:
                    out[level, here, :] = ends[side, f, level, near : near + 3, :]
                else:
                    out[level, here, :LANES] = ocean_ref[level, 0, strip_at]
                    out[level, here, LANES:] = ocean_ref[level, 1, strip_at]
            out[levels, here, :LANES] = strips[f, 0, strip_at, :]
            out[levels, here, LANES:] = strips[f, 1, strip_at, :]
            out[levels + 1, here, :LANES] = strips[f, 2, strip_at, :]
    low_out[...] = low[...].astype(BF16)
    high_out[...] = high[...].astype(BF16)


def outer_rows(west, east, ef, nf, ocean, own, spread):
    levels = ef.shape[0]
    edge = (levels + 2, 16, 2 * LANES)
    return pl.pallas_call(
        edges_body,
        name="outer_rows",
        out_shape=(
            jax.ShapeDtypeStruct(own.shape, F32),
            jax.ShapeDtypeStruct(own.shape[1:], F32),
            jax.ShapeDtypeStruct(edge, BF16),
            jax.ShapeDtypeStruct(edge, BF16),
        ),
        in_specs=[VMEM, VMEM, HBM, HBM] + [VMEM] * 3,
        out_specs=(VMEM,) * 4,
        scratch_shapes=[
            pltpu.VMEM(edge, F32),
            pltpu.VMEM(edge, F32),
            pltpu.VMEM((2, 2, levels, 8, 2 * LANES), F32),
            pltpu.SemaphoreType.DMA((2, 2)),
        ],
        compiler_params=pltpu.CompilerParams(vmem_limit_bytes=24 << 20),
    )(west, east, hbm(ef), hbm(nf), ocean, own, spread)


def place_body(
    odd_ref,
    arrived_ref,
    adj_hbm,
    ocean_ref,
    strip_ref,
    fields_ref,
    spread_ref,
    state_ref,
    out_strip_ref,
    swap_a_ref,
    swap_b_ref,
    adj_ref,
    hot,
    low,
    high,
    sems,
):
    devices = arrived_ref.shape[0]
    slots = devices * 8
    levels, rows = adj_ref.shape[1], adj_ref.shape[2]

    def arrival(level):
        return pltpu.make_async_copy(adj_hbm.at[:, level], adj_ref.at[:, level], sems.at[level])

    for level in range(levels):
        arrival(level).start()
    last = arrived_ref[:, levels].astype(F32).reshape(slots, LANES)
    heads = last.T[120:128]
    later = pltpu.roll(heads, 4, 1)
    row = fiota((rows, slots), 0)
    for b, source in enumerate((heads, later)):
        for c in range(2):
            found = source[0:1] == 2.0 * row + (c + 1.0)
            hot[pl.ds((2 * b + c) * rows, rows), :] = jnp.where(found, 1.0, 0.0).astype(BF16)
    lane = iota((slots, LANES), 1)
    mine = west_lane((slots, LANES))
    from_west = jnp.where(mine & (lane < 120), last, 0.0).astype(BF16)
    from_east = jnp.where(mine | (lane >= 120), 0.0, last).astype(BF16)
    spread = spread_ref[0]
    strips = dot(one_hot(rows, heads[1:2] - 1.0), dot(from_west, spread).astype(BF16)) + dot(
        one_hot(rows, heads[2:3] - 1.0), dot(from_east, spread).astype(BF16)
    )
    for tile in range(STRIPS):
        out_strip_ref[tile] = strip_ref[tile] + strips[:, tile * LANES : (tile + 1) * LANES]
    low[...] = jnp.zeros_like(low)
    high[...] = jnp.zeros_like(high)
    wide = iota((rows, LANES), 1)

    def one(level, carry):
        values = arrived_ref[:, level].astype(F32).reshape(slots, LANES).astype(BF16)
        arrival(level).wait()
        for t in range(2):
            k = t * levels + level
            tile, first = strip_of(k)
            ends = []
            for c in range(2):
                part = slice(c * LANES, (c + 1) * LANES)
                forced = dot(hot[pl.ds((2 * t + c) * rows, rows), :], values)
                total = adj_ref[t, level, :, part] + forced
                ends.append(total)
                masked = total * ocean_ref[level, c]
                state_ref[k, c] = masked
                low[level, 3 * t : 3 * t + 3, part] = masked[0:3]
                high[level, 3 * t : 3 * t + 3, part] = masked[rows - 3 : rows]
            held = out_strip_ref[tile]
            held = jnp.where(between(wide, first + 3, first + 9), turn(ends[0], first + 3), held)
            out_strip_ref[tile] = jnp.where(
                between(wide, first + 9, first + 15), turn(ends[1], first + 15), held
            )
        return carry

    lax.fori_loop(0, levels, one, 0)
    for tile in range(STRIPS):
        out_strip_ref[tile] = out_strip_ref[tile] * fields_ref[2, tile]
    for out, side in ((low, slice(0, 3)), (high, slice(rows - 3, rows))):
        out[levels, 0:3, :LANES] = out_strip_ref[0, side, :]
        out[levels, 0:3, LANES:] = out_strip_ref[1, side, :]
        out[levels, 3:6, :LANES] = out_strip_ref[2, side, :]
    odd = odd_ref[0] == 1
    swap_a_ref[...] = jnp.where(odd, low[...], high[...]).astype(BF16)
    swap_b_ref[...] = jnp.where(odd, high[...], low[...]).astype(BF16)


def place_records(odd, arrived, adj, ocean, strip, fields, spread):
    levels, rows, cells = adj.shape[1:]
    devices = arrived.shape[0]
    edge = jax.ShapeDtypeStruct((levels + 1, 8, cells), BF16)
    return pl.pallas_call(
        place_body,
        name="place_records",
        out_shape=(
            jax.ShapeDtypeStruct((2 * levels, 2, rows, LANES), F32),
            jax.ShapeDtypeStruct((STRIPS, rows, LANES), F32),
            edge,
            edge,
        ),
        in_specs=[SMEM, VMEM, HBM] + [VMEM] * 4,
        out_specs=(VMEM,) * 4,
        scratch_shapes=[
            pltpu.VMEM(adj.shape, F32),
            pltpu.VMEM((4 * rows, devices * 8), BF16),
            pltpu.VMEM(edge.shape, F32),
            pltpu.VMEM(edge.shape, F32),
            pltpu.SemaphoreType.DMA((levels,)),
        ],
        compiler_params=pltpu.CompilerParams(vmem_limit_bytes=24 << 20),
    )(odd, arrived, hbm(adj), ocean, strip, fields, spread)


def steps_body(
    where_ref,
    spread_ref,
    state_ref,
    strip_ref,
    swap_a_ref,
    swap_b_ref,
    ef_hbm,
    nf_hbm,
    ocean_ref,
    fields_ref,
    low_ref,
    high_ref,
    out_ref,
    flow_all,
    ocean,
    strip_flow,
    strip_ocean,
    coef,
    cells_a,
    cells_b,
    cells_c,
    patch,
    below,
    above,
    rows_low,
    rows_high,
    done,
    sems,
    level_sems,
):
    levels, rows = ocean_ref.shape[0], ocean_ref.shape[2]

    def arrivals(level):
        return [
            pltpu.make_async_copy(
                source.at[level, :, pl.ds(x * LANES, LANES)],
                flow_all.at[level, f, x, pl.ds(16, rows), :],
                level_sems.at[2 * f + x, level],
            )
            for f, source in enumerate((ef_hbm, nf_hbm))
            for x in range(2)
        ]

    for level in range(levels):
        for copy in arrivals(level):
            copy.start()
    tall = rows + 16
    inner = slice(16, 16 + rows)
    before, after = slice(13, 16), slice(16 + rows, 19 + rows)
    at_start, at_end, odd = where_ref[0], where_ref[1], where_ref[2] == 1
    lane, sub = iota((8, LANES), 1), iota((8, LANES), 0)
    for ref in (strip_flow.at[0], strip_flow.at[1], strip_ocean):
        ref[0, 0:16] = jnp.zeros((16, LANES), F32)
        ref[0, 16 + rows : 32 + rows] = jnp.zeros((16, LANES), F32)
    for x in range(2):
        ocean[x, 0:16] = jnp.zeros((16, LANES), F32)
        ocean[x, 16 + rows : 32 + rows] = jnp.zeros((16, LANES), F32)
    for ref in (cells_a, cells_b, cells_c):
        for t in range(2):
            for x in range(2):
                ref[t, x, 0:16] = jnp.zeros((16, LANES), F32)
                ref[t, x, 16 + rows : 32 + rows] = jnp.zeros((16, LANES), F32)
    below[...] = jnp.where(odd, swap_a_ref[...].astype(F32), swap_b_ref[...].astype(F32))
    above[...] = jnp.where(odd, swap_b_ref[...].astype(F32), swap_a_ref[...].astype(F32))
    rows_low[...] = low_ref[...].astype(F32)
    rows_high[...] = high_ref[...].astype(F32)
    top = 8 + rows
    shut_s = (sub == 0) & (at_start == 1)
    shut_n = (sub == 7) & (at_end == 1)

    def close_top(ref):
        ref[top : top + 8] = jnp.where(shut_n, 0.0, ref[top : top + 8])

    def prepare(x, i, flow, here, turned):
        at = slice(8 * i, 8 * i + 8)
        ce = jnp.maximum(here, 0.0)
        cw = -jnp.minimum(turned, 0.0)
        cn = jnp.maximum(flow[1, x, at], 0.0)
        cs = -jnp.minimum(flow[1, x, 8 * i - 1 : 8 * i + 7], 0.0)
        coef[0, x, at] = ce
        coef[1, x, at] = cw
        coef[2, x, at] = cn
        coef[3, x, at] = cs
        coef[4, x, at] = 1.0 - ce - cw - cn - cs

    def around_k(i, k):
        total = 4.0 * k
        if i == 2:
            total = total - jnp.where(shut_s, k, 0.0)
        if i == 1 + rows // 8:
            total = total - jnp.where(shut_n, k, 0.0)
        return total

    def update(source, x, i, k, here, east, west):
        at = slice(8 * i, 8 * i + 8)
        north = source[x, 8 * i + 1 : 8 * i + 9]
        south = source[x, 8 * i - 1 : 8 * i + 7]
        return (
            (coef[4, x, at] - around_k(i, k)) * here
            + (coef[0, x, at] + k) * east
            + (coef[1, x, at] + k) * west
            + (coef[2, x, at] + k) * north
            + (coef[3, x, at] + k) * south
        )

    def tiles(step):
        edge = 1 if step == STEPS - 1 else 0
        return range(1 + edge, 1 + tall // 8 - edge)

    for tile in range(STRIPS):
        k = jnp.zeros((1, LANES), F32)
        for s in range(7):
            slice_id = 7 * tile + s
            if slice_id < 2 * levels:
                own = between(iota((1, LANES), 1), 18 * s, 18 * s + 18)
                k = jnp.where(own, spread_ref[slice_id // levels, slice_id % levels], k)
        block = levels + tile // 2
        part = slice((tile % 2) * LANES, (tile % 2 + 1) * LANES)
        for f, dest in enumerate((strip_flow.at[0, 0], strip_flow.at[1, 0], strip_ocean.at[0])):
            dest[before] = rows_low[block, 3 * f : 3 * f + 3, part]
            dest[inner] = fields_ref[f, tile]
            dest[after] = rows_high[block, 3 * f : 3 * f + 3, part]
        close_top(strip_flow.at[1, 0])
        for i in range(1, 1 + tall // 8):
            face = strip_flow[0, 0, 8 * i : 8 * i + 8]
            prepare(0, i, strip_flow, face, pltpu.roll(face, 1, 1))
        here = slice(3 * (tile // 2), 3 * (tile // 2) + 3)
        cells_a[0, 0, before] = below[levels, here, part]
        cells_a[0, 0, inner] = strip_ref[tile]
        cells_a[0, 0, after] = above[levels, here, part]
        source = cells_a.at[0]
        for step in range(STEPS):
            dest = (cells_b, cells_c, None)[step]
            for i in tiles(step):
                at = slice(8 * i, 8 * i + 8)
                value = source[0, at]
                total = update(
                    source, 0, i, k, value, pltpu.roll(value, LANES - 1, 1), pltpu.roll(value, 1, 1)
                )
                if dest is None:
                    patch[tile, 8 * i - 16 : 8 * i - 8] = total
                else:
                    dest[0, 0, at] = total * strip_ocean[0, at]
            source = dest.at[0] if dest is not None else None

    def copies(level, slot):
        return [
            pltpu.make_async_copy(done.at[slot, t], out_ref.at[t, level], sems.at[slot, t])
            for t in range(2)
        ]

    def one(level, carry):
        flow = flow_all.at[level]
        for copy in arrivals(level):
            copy.wait()
        for f in range(2):
            for x in range(2):
                flow[f, x, 0:16] = jnp.zeros((16, LANES), F32)
                flow[f, x, 16 + rows : 32 + rows] = jnp.zeros((16, LANES), F32)
        for x in range(2):
            part = slice(x * LANES, (x + 1) * LANES)
            ocean[x, inner] = ocean_ref[level, x]
            for f, dest in enumerate((flow.at[0, x], flow.at[1, x], ocean.at[x])):
                dest[before] = rows_low[level, 3 * f : 3 * f + 3, part]
                dest[after] = rows_high[level, 3 * f : 3 * f + 3, part]
            close_top(flow.at[1, x])
            for t in range(2):
                cells_a[t, x, before] = below[level, 3 * t : 3 * t + 3, part]
                cells_a[t, x, inner] = state_ref[t * levels + level, x]
                cells_a[t, x, after] = above[level, 3 * t : 3 * t + 3, part]
        for i in range(1, 1 + tall // 8):
            at = slice(8 * i, 8 * i + 8)
            faces = [flow[0, x, at] for x in range(2)]
            turned = [pltpu.roll(v, 1, 1) for v in faces]
            turned[1] = jnp.where(lane == 0, turned[0], turned[1])
            for x in range(2):
                prepare(x, i, flow, faces[x], turned[x])
        slot = lax.rem(level, 2)

        @pl.when(level >= 2)
        def _():
            for copy in copies(level - 2, slot):
                copy.wait()

        ks = [spread_ref[t, level] for t in range(2)]
        spots = [strip_of(t * levels + level) for t in range(2)]
        buffers = (cells_a, cells_b, cells_c)
        for step in range(STEPS):
            for i in tiles(step):
                at = slice(8 * i, 8 * i + 8)
                for t in range(2):
                    source = buffers[step].at[t]
                    here = [source[x, at] for x in range(2)]
                    right = [pltpu.roll(v, LANES - 1, 1) for v in here]
                    left = [pltpu.roll(v, 1, 1) for v in here]
                    east = [jnp.where(lane == LANES - 1, right[1], right[0]), right[1]]
                    west = [left[0], jnp.where(lane == 0, left[0], left[1])]
                    for x in range(2):
                        total = update(source, x, i, ks[t], here[x], east[x], west[x])
                        if step < STEPS - 1:
                            buffers[step + 1][t, x, at] = total * ocean[x, at]
                            continue
                        tile, first = spots[t]
                        shift, keep = (125 - first, lane < 3) if x == 0 else (113 - first, lane >= 125)
                        fixed = turn(patch[tile, 8 * i - 16 : 8 * i - 8], shift)
                        done[slot, t, 8 * i - 16 : 8 * i - 8, x * LANES : (x + 1) * LANES] = (
                            jnp.where(keep, fixed, total)
                        )
        for copy in copies(level, slot):
            copy.start()
        return carry

    lax.fori_loop(0, levels, one, 0)
    for level in (levels - 2, levels - 1):
        for copy in copies(level, level % 2):
            copy.wait()


def run_steps(where, spread, state, strip, swap_a, swap_b, ef, nf, ocean, fields, low, high):
    levels, rows = ocean.shape[0], ocean.shape[2]
    tall, width = rows + 32, 2 * LANES
    buffer = pltpu.VMEM((2, 2, tall, LANES), F32)
    return pl.pallas_call(
        steps_body,
        name="three_steps",
        out_shape=jax.ShapeDtypeStruct((2, levels, rows, width), F32),
        in_specs=[SMEM, SMEM] + [VMEM] * 4 + [HBM] * 2 + [VMEM] * 4,
        out_specs=HBM,
        scratch_shapes=[
            pltpu.VMEM((levels, 2, 2, tall, LANES), F32),
            pltpu.VMEM((2, tall, LANES), F32),
            pltpu.VMEM((2, 1, tall, LANES), F32),
            pltpu.VMEM((1, tall, LANES), F32),
            pltpu.VMEM((5, 2, tall, LANES), F32),
            buffer,
            buffer,
            buffer,
            pltpu.VMEM((STRIPS, rows, LANES), F32),
            pltpu.VMEM(swap_a.shape, F32),
            pltpu.VMEM(swap_a.shape, F32),
            pltpu.VMEM(low.shape, F32),
            pltpu.VMEM(low.shape, F32),
            pltpu.VMEM((2, 2, rows, width), F32),
            pltpu.SemaphoreType.DMA((2, 2)),
            pltpu.SemaphoreType.DMA((4, levels)),
        ],
        compiler_params=pltpu.CompilerParams(vmem_limit_bytes=24 << 20),
    )(where, spread, state, strip, swap_a, swap_b, hbm(ef), hbm(nf), ocean, fields, low, high)


def around(block, axis, distance):
    count = lax.axis_size(axis)
    return lax.ppermute(block, axis, [(i, (i + distance) % count) for i in range(count)])


def along(block, axis, distance):
    count = lax.axis_size(axis)
    route = [(i, i + distance) for i in range(count) if 0 <= i + distance < count]
    return lax.ppermute(block, axis, route)


def swapped(block, axis, start):
    count = lax.axis_size(axis)
    lower = range(start, count - 1, 2)
    return lax.ppermute(block, axis, [(i, i + 1) for i in lower] + [(i + 1, i) for i in lower])


def per_device(
    adjoint_in,
    east_flow,
    north_flow,
    diffusivity,
    land_mask,
    forcing,
    obs_tile,
    obs_block,
    obs_live,
):
    n_lat, n_lon = lax.axis_size("lat"), lax.axis_size("lon")
    lat = lax.axis_index("lat")
    odd = lat % 2
    where = jnp.stack([lat == 0, lat == n_lat - 1, odd == 1]).astype(jnp.int32)
    packed = pack_records(
        forcing.transpose(0, 1, 3, 2, 4), obs_tile, obs_block, obs_live, n_lat * n_lon, n_lon
    )
    arrived = lax.all_to_all(packed, ("lat", "lon"), split_axis=0, concat_axis=0, tiled=True)
    columns, ocean = outer_columns(adjoint_in, east_flow, north_flow, land_mask)
    west = around(columns, "lon", 1)
    east = around(columns, "lon", -1)
    own, spread = own_strips(east_flow, north_flow, ocean)
    fields, adj_strip, low, high = outer_rows(
        west, east, east_flow, north_flow, ocean, own, spread
    )
    below = along(high, "lat", 1)
    above = along(low, "lat", -1)
    state, strip, swap_a, swap_b = place_records(
        odd.reshape(1).astype(jnp.int32), arrived, adjoint_in, ocean, adj_strip, fields, spread
    )
    swap_a = swapped(swap_a, "lat", 0)
    swap_b = swapped(swap_b, "lat", 1)
    return run_steps(
        where,
        diffusivity,
        state,
        strip,
        swap_a,
        swap_b,
        east_flow,
        north_flow,
        ocean,
        fields,
        below,
        above,
    )


def solution(mesh):
    in_specs = (
        P(None, None, "lat", "lon"),
        P(None, "lat", "lon"),
        P(None, "lat", "lon"),
        P(),
        P(None, "lat", "lon"),
        P(("lat", "lon"), None, None, None, None),
        P(("lat", "lon"), None),
        P(("lat", "lon"), None),
        P(("lat", "lon")),
    )
    out_specs = P(None, None, "lat", "lon")
    return jax.shard_map(
        per_device, mesh=mesh, in_specs=in_specs, out_specs=out_specs, check_vma=False
    )
```

profile of v0, /device:TPU:8, one launch (start us, length us, event | category | flops | bytes accessed | tf_op | source)
XLA Modules:
  0.0 49.6 jit_solution(15722030344393901409)
XLA Ops:
  0.7 2.6 %pack_records.1 = bf16[32,11,8,128]{3,2,1,0:T(8,128)(2,1)} custom-call(s32[1]{0:T(128)S(6)} %copy.10.live_ref, s32[1,64]{1,0:T(1,128)} %tile_in.1, s32[1,64]{1,0:T(1,128)} %block_in.1, bf16[1,64,10,2,128]{4,3,2,1,0:T(2,128)(2,1)} %bitcast.5), custom_call_target="tpu_custom_call" | custom-call | tf_op jit(solution)/shard_map/pack_records/pallas_call | solution.py:129
  3.3 6.0 %all-to-all-start = ((bf16[32,11,8,128]{3,2,1,0:T(8,128)(2,1)}), bf16[32,11,8,128]{3,2,1,0:T(8,128)(2,1)S(1)}, u32[]{:S(2)}, u32[]{:S(2)}) async-start(bf16[32,11,8,128]{3,2,1,0:T(8,128)(2,1)} %pack_records.1), calls=%async_computation | async-start | bytes 1441792 | tf_op jit(solution)/shard_map/all_to_all | solution.py:776
  9.3 3.7 %outer_columns.1 = (bf16[128,384]{1,0:T(8,128)(2,1)S(1)}, f32[10,2,128,128]{3,2,1,0:T(8,128)S(1)}) custom-call(f32[2,10,128,256]{3,2,1,0:T(8,128)} %adj_hbm.3, f32[10,128,256]{2,1,0:T(8,128)} %ef_hbm.7, f32[10,128,256]{2,1,0:T(8,128)} %nf_hbm.7, s32[10,128,256]{2,1,0:T(8,128)} %mask_hbm.1), custom_call_target="tpu_custom_call" | custom-call | tf_op jit(solution)/shard_map/outer_columns/pallas_call | solution.py:220
  13.0 2.2 %collective-permute-start.1 = (bf16[128,384]{1,0:T(8,128)(2,1)S(1)}, bf16[128,384]{1,0:T(8,128)(2,1)S(1)}, u32[]{:S(2)}, u32[]{:S(2)}) collective-permute-start(bf16[128,384]{1,0:T(8,128)(2,1)S(1)} %get-tuple-element.18), channel_id=1, source_target_pairs={{0,7},{1,0},{2,1},{3,2},{4,3},{5,4},{6,5},{7,6},{8,15},{9,8},{10,9... | collective-permute-start | bytes 294920 | tf_op jit(solution)/shard_map/ppermute | solution.py:743
  15.2 0.0 collective-permute-start
  15.2 5.4 %own_strips.1 = (f32[3,3,128,128]{3,2,1,0:T(8,128)S(1)}, bf16[3,128,384]{2,1,0:T(8,128)(2,1)S(1)}) custom-call(f32[10,128,256]{2,1,0:T(8,128)} %ef_hbm.7, f32[10,128,256]{2,1,0:T(8,128)} %nf_hbm.7, f32[10,2,128,128]{3,2,1,0:T(8,128)S(1)} %get-tuple-element.17.ocean_ref), custom_call_target="tpu_custom_call" | custom-call | flops 100000000 | bytes 10000000 | tf_op jit(solution)/shard_map/own_strips/pallas_call | solution.py:289
  20.6 0.0 collective-permute-done.1.east
  20.6 0.9 %collective-permute-done.west = bf16[128,384]{1,0:T(8,128)(2,1)S(1)} collective-permute-done((bf16[128,384]{1,0:T(8,128)(2,1)S(1)}, bf16[128,384]{1,0:T(8,128)(2,1)S(1)}, u32[]{:S(2)}, u32[]{:S(2)}) %collective-permute-start) | collective-permute-done | bytes 98336 | tf_op jit(solution)/shard_map/ppermute | solution.py:743
  21.6 1.2 %outer_rows.1 = (f32[3,3,128,128]{3,2,1,0:T(8,128)S(1)}, f32[3,128,128]{2,1,0:T(8,128)S(1)}, bf16[12,16,256]{2,1,0:T(8,128)(2,1)S(1)}, bf16[12,16,256]{2,1,0:T(8,128)(2,1)S(1)}) custom-call(bf16[128,384]{1,0:T(8,128)(2,1)S(1)} %collective-permute-done.west, bf16[128,384]{1,0:T(8,128)(2,1)S(1)} %collective-permute-done.1.east, f32[10,128,256]{2,1,0:T(8,128)} %ef_hbm.7, ...), custom_call_target="tpu_custom_call" | custom-call | tf_op jit(solution)/shard_map/outer_rows/pallas_call | solution.py:359
  22.8 2.7 %collective-permute-start.4 = (bf16[12,16,256]{2,1,0:T(8,128)(2,1)S(1)}, bf16[12,16,256]{2,1,0:T(8,128)(2,1)S(1)}, u32[]{:S(2)}, u32[]{:S(2)}) collective-permute-start(bf16[12,16,256]{2,1,0:T(8,128)(2,1)S(1)} %get-tuple-element.27), channel_id=1, source_target_pairs={{0,8},{8,16},{16,24},{1,9},{9,17},{17,25},{2,10},{10,18},{18,26},{... | collective-permute-start | bytes 294920 | tf_op jit(solution)/shard_map/ppermute | solution.py:749
  25.5 3.1 %collective-permute-start.5 = (bf16[12,16,256]{2,1,0:T(8,128)(2,1)S(1)}, bf16[12,16,256]{2,1,0:T(8,128)(2,1)S(1)}, u32[]{:S(2)}, u32[]{:S(2)}) collective-permute-start(bf16[12,16,256]{2,1,0:T(8,128)(2,1)S(1)} %get-tuple-element.28), channel_id=1, source_target_pairs={{8,0},{16,8},{24,16},{9,1},{17,9},{25,17},{10,2},{18,10},{26,18},{... | collective-permute-start | bytes 294920 | tf_op jit(solution)/shard_map/ppermute | solution.py:749
  28.6 0.0 all-to-all-done.arrived_ref
  28.6 0.0 copy-start
  28.6 4.0 %place_records.1 = (f32[20,2,128,128]{3,2,1,0:T(8,128)S(1)}, f32[3,128,128]{2,1,0:T(8,128)S(1)}, bf16[11,8,256]{2,1,0:T(8,128)(2,1)S(1)}, bf16[11,8,256]{2,1,0:T(8,128)(2,1)S(1)}) custom-call(s32[1]{0:T(128)} %bitcast.3.odd_ref, bf16[32,11,8,128]{3,2,1,0:T(8,128)(2,1)S(1)} %all-to-all-done.arrived_ref, f32[2,10,128,256]{3,2,1,0:T(8,128)} %adj_hbm.3, ...), custom_call_target="tpu_custom_call" | custom-call | tf_op jit(solution)/shard_map/place_records/pallas_call | solution.py:468
  32.6 0.2 collective-permute-start.2
  32.8 3.9 %collective-permute-start.3 = (bf16[11,8,256]{2,1,0:T(8,128)(2,1)S(1)}, bf16[11,8,256]{2,1,0:T(8,128)(2,1)S(1)}, u32[]{:S(2)}, u32[]{:S(2)}) collective-permute-start(bf16[11,8,256]{2,1,0:T(8,128)(2,1)S(1)} %get-tuple-element.26), channel_id=1, source_target_pairs={{8,16},{16,8},{9,17},{17,9},{10,18},{18,10},{11,19},{19,11},{12,20... | collective-permute-start | bytes 135176 | tf_op jit(solution)/shard_map/ppermute | solution.py:755
  36.7 0.1 add_convert_fusion.where_ref
  36.8 0.0 collective-permute-done.4.low_ref
  36.8 0.0 collective-permute-done.5.high_ref
  36.8 0.0 collective-permute-done.2.swap_a_ref
  36.8 2.0 %collective-permute-done.3.swap_b_ref = bf16[11,8,256]{2,1,0:T(8,128)(2,1)S(1)} collective-permute-done((bf16[11,8,256]{2,1,0:T(8,128)(2,1)S(1)}, bf16[11,8,256]{2,1,0:T(8,128)(2,1)S(1)}, u32[]{:S(2)}, u32[]{:S(2)}) %collective-permute-start.3) | collective-permute-done | bytes 45088 | tf_op jit(solution)/shard_map/ppermute | solution.py:755
  38.8 0.0 copy-done
  38.8 10.9 %three_steps.1 = f32[2,10,128,256]{3,2,1,0:T(8,128)} custom-call(s32[3]{0:T(128)S(1)} %add_convert_fusion.where_ref, f32[2,10]{1,0:T(2,128)S(1)} %copy-done, f32[20,2,128,128]{3,2,1,0:T(8,128)S(1)} %get-tuple-element.23.state_ref, f32[3,128,128]{2,1,0:T(8,128)S(1)} %get-tuple-element.24.strip_ref, bf16[11,8,256]{2,1,0:T(8,128)(2,1)S(1)} %collective-permute-done.2.swap_a_ref, ...), custom_call_target="tpu_custom_call" | custom-call | tf_op jit(solution)/shard_map/three_steps/pallas_call | solution.py:713
Async XLA Ops:
  3.3 25.3 %all-to-all-start = ((bf16[32,11,8,128]{3,2,1,0:T(8,128)(2,1)}), bf16[32,11,8,128]{3,2,1,0:T(8,128)(2,1)S(1)}, u32[]{:S(2)}, u32[]{:S(2)}) async-start(bf16[32,11,8,128]{3,2,1,0:T(8,128)(2,1)} %pack_records.1), calls=%async_computation | async-start | bytes 1441792 | tf_op jit(solution)/shard_map/all_to_all | solution.py:776
  13.0 7.6 %collective-permute-start.1 = (bf16[128,384]{1,0:T(8,128)(2,1)S(1)}, bf16[128,384]{1,0:T(8,128)(2,1)S(1)}, u32[]{:S(2)}, u32[]{:S(2)}) collective-permute-start(bf16[128,384]{1,0:T(8,128)(2,1)S(1)} %get-tuple-element.18), channel_id=1, source_target_pairs={{0,7},{1,0},{2,1},{3,2},{4,3},{5,4},{6,5},{7,6},{8,15},{9,8},{10,9... | collective-permute-start | bytes 294920 | tf_op jit(solution)/shard_map/ppermute | solution.py:743
  15.2 6.4 %collective-permute-start = (bf16[128,384]{1,0:T(8,128)(2,1)S(1)}, bf16[128,384]{1,0:T(8,128)(2,1)S(1)}, u32[]{:S(2)}, u32[]{:S(2)}) collective-permute-start(bf16[128,384]{1,0:T(8,128)(2,1)S(1)} %get-tuple-element.18), channel_id=1, source_target_pairs={{0,1},{1,2},{2,3},{3,4},{4,5},{5,6},{6,7},{7,0},{8,9},{9,10},{10,1... | collective-permute-start | bytes 294920 | tf_op jit(solution)/shard_map/ppermute | solution.py:743
  22.8 14.0 %collective-permute-start.4 = (bf16[12,16,256]{2,1,0:T(8,128)(2,1)S(1)}, bf16[12,16,256]{2,1,0:T(8,128)(2,1)S(1)}, u32[]{:S(2)}, u32[]{:S(2)}) collective-permute-start(bf16[12,16,256]{2,1,0:T(8,128)(2,1)S(1)} %get-tuple-element.27), channel_id=1, source_target_pairs={{0,8},{8,16},{16,24},{1,9},{9,17},{17,25},{2,10},{10,18},{18,26},{... | collective-permute-start | bytes 294920 | tf_op jit(solution)/shard_map/ppermute | solution.py:749
  25.5 11.3 %collective-permute-start.5 = (bf16[12,16,256]{2,1,0:T(8,128)(2,1)S(1)}, bf16[12,16,256]{2,1,0:T(8,128)(2,1)S(1)}, u32[]{:S(2)}, u32[]{:S(2)}) collective-permute-start(bf16[12,16,256]{2,1,0:T(8,128)(2,1)S(1)} %get-tuple-element.28), channel_id=1, source_target_pairs={{8,0},{16,8},{24,16},{9,1},{17,9},{25,17},{10,2},{18,10},{26,18},{... | collective-permute-start | bytes 294920 | tf_op jit(solution)/shard_map/ppermute | solution.py:749
  28.6 10.1 %copy-start = (f32[2,10]{1,0:T(2,128)S(1)}, f32[2,10]{1,0:T(2,128)}, u32[]{:S(2)}) copy-start(f32[2,10]{1,0:T(2,128)} %spread_ref.1) | copy-start | bytes 244
  32.6 4.2 %collective-permute-start.2 = (bf16[11,8,256]{2,1,0:T(8,128)(2,1)S(1)}, bf16[11,8,256]{2,1,0:T(8,128)(2,1)S(1)}, u32[]{:S(2)}, u32[]{:S(2)}) collective-permute-start(bf16[11,8,256]{2,1,0:T(8,128)(2,1)S(1)} %get-tuple-element.25), channel_id=1, source_target_pairs={{0,8},{16,24},{8,0},{24,16},{1,9},{17,25},{9,1},{25,17},{2,10},{18... | collective-permute-start | bytes 135176 | tf_op jit(solution)/shard_map/ppermute | solution.py:755
  32.8 5.9 %collective-permute-start.3 = (bf16[11,8,256]{2,1,0:T(8,128)(2,1)S(1)}, bf16[11,8,256]{2,1,0:T(8,128)(2,1)S(1)}, u32[]{:S(2)}, u32[]{:S(2)}) collective-permute-start(bf16[11,8,256]{2,1,0:T(8,128)(2,1)S(1)} %get-tuple-element.26), channel_id=1, source_target_pairs={{8,16},{16,8},{9,17},{17,9},{10,18},{18,10},{11,19},{19,11},{12,20... | collective-permute-start | bytes 135176 | tf_op jit(solution)/shard_map/ppermute | solution.py:755
where the time goes:
time: 50.5 us; the launch traced here: 49.6 us
  Pallas kernels  27.8 us (55%)
  starting transfers between devices  18.1 us (36%)
  waiting for transfers between devices  2.92 us (6%)
  between operations  0.76 us (2%)
    pallas_call x1, Pallas kernels, run_steps(): pl.pallas_call(steps_body, name='three_steps', out_shape=jax.ShapeDtypeSt...  10.9 us
    all_to_all x1, starting transfers between devices, per_device(): lax.all_to_all(packed, ('lat', 'lon'), split_axis=0, concat_axis=0, tiled...  6.05 us
    ppermute x2, starting transfers between devices, along(): return lax.ppermute(block, axis, route)  5.84 us
    pallas_call x1, Pallas kernels, own_strips(): pl.pallas_call(own_body, name='own_strips', out_shape=(jax.ShapeDtypeStru...  5.44 us
    ppermute x2, starting transfers between devices, swapped(): lax.ppermute(block, axis, [(i, i + 1) for i in lower] + [(i + 1, i) for i...  4.06 us
    pallas_call x1, Pallas kernels, place_records(): pl.pallas_call(place_body, name='place_records', out_shape=(jax.ShapeDtyp...  3.99 us
    pallas_call x1, Pallas kernels, outer_columns(): pl.pallas_call(columns_body, name='outer_columns', out_shape=(jax.ShapeDt...  3.66 us
    pallas_call x1, Pallas kernels, pack_records(): pl.pallas_call(functools.partial(pack_body, n_lon), name='pack_records',...  2.63 us
  transfers between devices with their start and end apart: 7, of which 2 were waited for; matrix products, arithmetic and copies ran while one was open for 0% of the time, Pallas kernels for 29%

commit v1 on v0

--- a/solution.py
+++ b/solution.py
@@ -9,6 +9,7 @@
 
 STEPS = 3
 LANES = 128
+KEPT = 9
 F32 = jnp.float32
 BF16 = jnp.bfloat16
 HBM = pl.BlockSpec(memory_space=pltpu.HBM)
@@ -42,9 +43,9 @@
     n_lon, live_ref, tile_in, block_in, forcing_in, out_hbm,
     tile_ref, block_ref, forcing_ref, out_ref, wide, sems, out_sems,
 ):
-    records, levels = forcing_ref.shape[1], forcing_ref.shape[2]
-    count = 2 * levels
-    devices = out_ref.shape[0]
+    records, devices = tile_ref.shape[1], out_ref.shape[0]
+    count = forcing_ref.shape[0] // records
+    levels = count // 2
     moves = [
         pltpu.make_async_copy(source, dest, sems.at[i])
         for i, (source, dest) in enumerate(
@@ -77,13 +78,7 @@
     to_east = jnp.where(live & (half == 1.0), east * 8.0 + rank, -8.0)
     to_west = jnp.where(live & (half == 0.0), west * 8.0 + rank, -8.0)
     moves[2].wait()
-
-    def widen(r, carry):
-        for level in range(levels):
-            wide[pl.ds(r * count + 2 * level, 2), :] = forcing_ref[0, r, level].astype(F32)
-        return carry
-
-    lax.fori_loop(0, records, widen, 0, unroll=4)
+    wide[...] = forcing_ref[...].astype(F32)
     sent = []
 
     def send(q, values):
@@ -124,7 +119,8 @@
 
 
 def pack_records(forcing, tile, block, live, devices, n_lon):
-    records, levels, width = forcing.shape[1], forcing.shape[2], forcing.shape[4]
+    records, width = tile.shape[1], forcing.shape[1]
+    levels = forcing.shape[0] // records // 2
     out = (devices, levels + 1, 8, width)
     return pl.pallas_call(
         functools.partial(pack_body, n_lon),
@@ -137,7 +133,7 @@
             pltpu.VMEM(block.shape, jnp.int32),
             pltpu.VMEM(forcing.shape, BF16),
             pltpu.VMEM(out, BF16),
-            pltpu.VMEM((records * levels * 2, width), F32),
+            pltpu.VMEM(forcing.shape, F32),
             pltpu.SemaphoreType.DMA((3,)),
             pltpu.SemaphoreType.DMA((levels + 1,)),
         ],
@@ -202,12 +198,12 @@
         for copy in moves(level):
             copy.wait()
         for x in range(2):
-            ocean_ref[level, x] = mask[level, :, x * LANES : (x + 1) * LANES].astype(F32)
+            ocean_ref[level, x] = mask[level, :, x * LANES : (x + 1) * LANES].astype(F32).astype(BF16)
         for t in range(2):
             put(0, t * levels + level, adj_ref[t, level, :, :LANES], adj_ref[t, level, :, LANES:])
         put(1, level, flow_ref[level, 0, 0], flow_ref[level, 0, 1])
         put(1, levels + level, flow_ref[level, 1, 0], flow_ref[level, 1, 1])
-        put(2, level, ocean_ref[level, 0], ocean_ref[level, 1])
+        put(2, level, mask[level, :, :LANES].astype(F32), mask[level, :, LANES:].astype(F32))
         return carry
 
     lax.fori_loop(0, levels, one, 0)
@@ -222,7 +218,7 @@
         name="outer_columns",
         out_shape=(
             jax.ShapeDtypeStruct((rows, 3 * LANES), BF16),
-            jax.ShapeDtypeStruct((levels, 2, rows, LANES), F32),
+            jax.ShapeDtypeStruct((levels, 2, rows, LANES), BF16),
         ),
         in_specs=[HBM] * 4,
         out_specs=(VMEM,) * 2,
@@ -237,7 +233,11 @@
     )(*map(hbm, (adj, ef, nf, mask)))
 
 
-def own_body(ef_hbm, nf_hbm, ocean_ref, strips, spread_ref, flow_ref, sems):
+def own_body(
+    ef_hbm, nf_hbm, adj_hbm, ocean_ref,
+    strips, spread_ref, rest_ref, first_ref, low_out, high_out,
+    flow_ref, low, high, sems, adj_sem,
+):
     levels, rows = ocean_ref.shape[0], ocean_ref.shape[2]
 
     def moves(level):
@@ -254,8 +254,9 @@
     for level in range(levels):
         for copy in moves(level):
             copy.start()
-    square = (LANES, LANES)
-    source, target = fiota(square, 0), fiota(square, 1)
+    fetch = pltpu.make_async_copy(adj_hbm.at[0, pl.ds(0, KEPT)], first_ref, adj_sem)
+    fetch.start()
+    source, target = fiota((LANES, LANES), 0), fiota((1, LANES), 1)
     order = jnp.floor((target + 0.5) / 18.0)
     offset = target - 18.0 * order
     inner = jnp.where(offset < 3.0, offset, offset - 12.0)
@@ -265,121 +266,123 @@
         level = jnp.where(k < levels, k, k - levels)
         live = used & (k < 2.0 * levels)
         for m, place in enumerate((k, level, level + levels)):
-            hit = live & (source == 6.0 * place + inner)
-            spread_ref[m, :, tile * LANES : (tile + 1) * LANES] = jnp.where(hit, 1.0, 0.0).astype(BF16)
+            hit = source == jnp.where(live, 6.0 * place + inner, -1.0)
+            part = slice(tile * LANES, (tile + 1) * LANES)
+            ones = jnp.where(hit, 1.0, 0.0).astype(BF16)
+            if m == 0:
+                spread_ref[:, part] = ones
+            else:
+                rest_ref[m - 1, :, part] = ones
     strips[...] = jnp.zeros_like(strips)
+    low[...] = jnp.zeros_like(low)
+    high[...] = jnp.zeros_like(high)
     lane = iota((rows, LANES), 1)
 
     def one(level, carry):
         for copy in moves(level):
             copy.wait()
         for f, ref in enumerate((flow_ref.at[level, 0], flow_ref.at[level, 1], ocean_ref.at[level])):
-            own = jnp.where(lane < 9, turn(ref[0], 3), turn(ref[1], 15))
+            ends = [ref[x].astype(F32) for x in range(2)]
+            for x in range(2):
+                here = slice(x * LANES, (x + 1) * LANES)
+                low[level, 3 * f : 3 * f + 3, here] = ends[x][0:3]
+                high[level, 3 * f : 3 * f + 3, here] = ends[x][rows - 3 : rows]
+            own = jnp.where(lane < 9, turn(ends[0], 3), turn(ends[1], 15))
             for t in range(2):
                 tile, first = strip_of(t * levels + level)
                 keep = between(lane, first + 3, first + 15)
                 strips[f, tile] = jnp.where(keep, turn(own, first), strips[f, tile])
         return carry
 
-    lax.fori_loop(0, levels, one, 0)
-
-
-def own_strips(ef, nf, ocean):
+    for level in range(levels):
+        one(level, 0)
+    low_out[...] = low[...].astype(BF16)
+    high_out[...] = high[...].astype(BF16)
+    fetch.wait()
+
+
+def own_strips(ef, nf, adj, ocean):
     levels, rows = ef.shape[0], ef.shape[1]
     return pl.pallas_call(
         own_body,
         name="own_strips",
         out_shape=(
             jax.ShapeDtypeStruct((3, STRIPS, rows, LANES), F32),
-            jax.ShapeDtypeStruct((3, LANES, STRIPS * LANES), BF16),
+            jax.ShapeDtypeStruct((LANES, STRIPS * LANES), BF16),
+            jax.ShapeDtypeStruct((2, LANES, STRIPS * LANES), BF16),
+            jax.ShapeDtypeStruct((KEPT,) + adj.shape[2:], F32),
+            jax.ShapeDtypeStruct((levels, 16, 2 * LANES), BF16),
+            jax.ShapeDtypeStruct((levels, 16, 2 * LANES), BF16),
         ),
-        in_specs=[HBM, HBM, VMEM],
-        out_specs=(VMEM, VMEM),
+        in_specs=[HBM, HBM, HBM, VMEM],
+        out_specs=(VMEM,) * 6,
         scratch_shapes=[
             pltpu.VMEM((levels, 2, 2, rows, LANES), F32),
+            pltpu.VMEM((levels, 16, 2 * LANES), F32),
+            pltpu.VMEM((levels, 16, 2 * LANES), F32),
             pltpu.SemaphoreType.DMA((4, levels)),
+            pltpu.SemaphoreType.DMA,
         ],
         cost_estimate=pl.CostEstimate(flops=10**8, bytes_accessed=10**7, transcendentals=0),
         compiler_params=pltpu.CompilerParams(vmem_limit_bytes=24 << 20),
-    )(hbm(ef), hbm(nf), ocean)
+    )(hbm(ef), hbm(nf), hbm(adj), ocean)
 
 
 def edges_body(
-    west, east, ef_hbm, nf_hbm, ocean_ref, own_ref, spread_ref,
-    strips, adj, low_out, high_out, low, high, ends, sems,
+    west, east, own_ref, spread_ref, rest_ref, low_main, high_main,
+    strips, adj, low_out, high_out, held,
 ):
-    levels, rows = ocean_ref.shape[0], ocean_ref.shape[2]
-    copies = [
-        pltpu.make_async_copy(
-            source.at[:, pl.ds(base, 8), :], ends.at[side, f], sems.at[side, f]
-        )
-        for side, base in ((0, 0), (1, rows - 8))
-        for f, source in enumerate((ef_hbm, nf_hbm))
-    ]
-    for copy in copies:
-        copy.start()
-    low[...] = jnp.zeros_like(low)
-    high[...] = jnp.zeros_like(high)
+    levels, rows = low_main.shape[0], own_ref.shape[2]
 
     def halo(tile, m):
         part = slice(tile * LANES, (tile + 1) * LANES)
         theirs, ours = west[:, part].astype(F32), east[:, part].astype(F32)
         merged = jnp.where(west_lane(theirs.shape), theirs, ours).astype(BF16)
-        return dot(merged, spread_ref[m])
-
-    halos = halo(0, 0)
-    for tile in range(STRIPS):
-        adj[tile] = halos[:, tile * LANES : (tile + 1) * LANES]
+        return dot(merged, rest_ref[m - 1] if m else spread_ref[...])
+
     for f, (source, m) in enumerate(((1, 1), (1, 2), (2, 1))):
         halos = halo(source, m)
         for tile in range(STRIPS):
             strips[f, tile] = own_ref[f, tile] + halos[:, tile * LANES : (tile + 1) * LANES]
-    for copy in copies:
-        copy.wait()
-    for side, (out, first, near) in enumerate(((low, 0, 0), (high, rows - 3, 5))):
-        strip_at = slice(first, first + 3)
+    halos = halo(0, 0)
+    for tile in range(STRIPS):
+        adj[tile] = halos[:, tile * LANES : (tile + 1) * LANES].astype(BF16)
+    held[...] = jnp.zeros_like(held)
+    for side, (out, main, first) in enumerate(
+        ((low_out, low_main, 0), (high_out, high_main, rows - 3))
+    ):
+        at = slice(first, first + 3)
         for f in range(3):
             here = slice(3 * f, 3 * f + 3)
-            for level in range(levels):
-                if f < 2:
-                    out[level, here, :] = ends[side, f, level, near : near + 3, :]
-                else:
-                    out[level, here, :LANES] = ocean_ref[level, 0, strip_at]
-                    out[level, here, LANES:] = ocean_ref[level, 1, strip_at]
-            out[levels, here, :LANES] = strips[f, 0, strip_at, :]
-            out[levels, here, LANES:] = strips[f, 1, strip_at, :]
-            out[levels + 1, here, :LANES] = strips[f, 2, strip_at, :]
-    low_out[...] = low[...].astype(BF16)
-    high_out[...] = high[...].astype(BF16)
-
-
-def outer_rows(west, east, ef, nf, ocean, own, spread):
-    levels = ef.shape[0]
-    edge = (levels + 2, 16, 2 * LANES)
+            held[side, 0, here, :LANES] = strips[f, 0, at, :]
+            held[side, 0, here, LANES:] = strips[f, 1, at, :]
+            held[side, 1, here, :LANES] = strips[f, 2, at, :]
+        out[0:levels] = main[...]
+        out[levels : levels + 2] = held[side].astype(BF16)
+
+
+def outer_rows(west, east, own, spread, rest, low, high):
+    edge = (low.shape[0] + 2,) + low.shape[1:]
     return pl.pallas_call(
         edges_body,
         name="outer_rows",
         out_shape=(
             jax.ShapeDtypeStruct(own.shape, F32),
-            jax.ShapeDtypeStruct(own.shape[1:], F32),
+            jax.ShapeDtypeStruct(own.shape[1:], BF16),
             jax.ShapeDtypeStruct(edge, BF16),
             jax.ShapeDtypeStruct(edge, BF16),
         ),
-        in_specs=[VMEM, VMEM, HBM, HBM] + [VMEM] * 3,
+        in_specs=[VMEM] * 7,
         out_specs=(VMEM,) * 4,
-        scratch_shapes=[
-            pltpu.VMEM(edge, F32),
-            pltpu.VMEM(edge, F32),
-            pltpu.VMEM((2, 2, levels, 8, 2 * LANES), F32),
-            pltpu.SemaphoreType.DMA((2, 2)),
-        ],
+        scratch_shapes=[pltpu.VMEM((2, 2) + low.shape[1:], F32)],
         compiler_params=pltpu.CompilerParams(vmem_limit_bytes=24 << 20),
-    )(west, east, hbm(ef), hbm(nf), ocean, own, spread)
+    )(west, east, own, spread, rest, low, high)
 
 
 def place_body(
     odd_ref,
     arrived_ref,
+    first_ref,
     adj_hbm,
     ocean_ref,
     strip_ref,
@@ -389,7 +392,7 @@
     out_strip_ref,
     swap_a_ref,
     swap_b_ref,
-    adj_ref,
+    second_ref,
     hot,
     low,
     high,
@@ -397,13 +400,20 @@
 ):
     devices = arrived_ref.shape[0]
     slots = devices * 8
-    levels, rows = adj_ref.shape[1], adj_ref.shape[2]
-
-    def arrival(level):
-        return pltpu.make_async_copy(adj_hbm.at[:, level], adj_ref.at[:, level], sems.at[level])
-
-    for level in range(levels):
-        arrival(level).start()
+    levels, rows = ocean_ref.shape[0], first_ref.shape[1]
+    part = levels // 2
+    late = levels - KEPT
+    fetch = [
+        pltpu.make_async_copy(
+            adj_hbm.at[1, pl.ds(i * part, part)], second_ref.at[pl.ds(i * part, part)], sems.at[i]
+        )
+        for i in range(2)
+    ]
+    rest = pltpu.make_async_copy(
+        adj_hbm.at[0, pl.ds(KEPT, late)], second_ref.at[pl.ds(levels, late)], sems.at[2]
+    )
+    for copy in [rest] + fetch:
+        copy.start()
     last = arrived_ref[:, levels].astype(F32).reshape(slots, LANES)
     heads = last.T[120:128]
     later = pltpu.roll(heads, 4, 1)
@@ -416,40 +426,44 @@
     mine = west_lane((slots, LANES))
     from_west = jnp.where(mine & (lane < 120), last, 0.0).astype(BF16)
     from_east = jnp.where(mine | (lane >= 120), 0.0, last).astype(BF16)
-    spread = spread_ref[0]
+    spread = spread_ref[...]
     strips = dot(one_hot(rows, heads[1:2] - 1.0), dot(from_west, spread).astype(BF16)) + dot(
         one_hot(rows, heads[2:3] - 1.0), dot(from_east, spread).astype(BF16)
     )
     for tile in range(STRIPS):
-        out_strip_ref[tile] = strip_ref[tile] + strips[:, tile * LANES : (tile + 1) * LANES]
+        out_strip_ref[tile] = strip_ref[tile].astype(F32) + strips[:, tile * LANES : (tile + 1) * LANES]
     low[...] = jnp.zeros_like(low)
     high[...] = jnp.zeros_like(high)
     wide = iota((rows, LANES), 1)
 
-    def one(level, carry):
+    def one(t, level):
         values = arrived_ref[:, level].astype(F32).reshape(slots, LANES).astype(BF16)
-        arrival(level).wait()
-        for t in range(2):
-            k = t * levels + level
-            tile, first = strip_of(k)
-            ends = []
-            for c in range(2):
-                part = slice(c * LANES, (c + 1) * LANES)
-                forced = dot(hot[pl.ds((2 * t + c) * rows, rows), :], values)
-                total = adj_ref[t, level, :, part] + forced
-                ends.append(total)
-                masked = total * ocean_ref[level, c]
-                state_ref[k, c] = masked
-                low[level, 3 * t : 3 * t + 3, part] = masked[0:3]
-                high[level, 3 * t : 3 * t + 3, part] = masked[rows - 3 : rows]
-            held = out_strip_ref[tile]
-            held = jnp.where(between(wide, first + 3, first + 9), turn(ends[0], first + 3), held)
-            out_strip_ref[tile] = jnp.where(
-                between(wide, first + 9, first + 15), turn(ends[1], first + 15), held
-            )
-        return carry
-
-    lax.fori_loop(0, levels, one, 0)
+        k = t * levels + level
+        tile, first = strip_of(k)
+        ends = []
+        for c in range(2):
+            part = slice(c * LANES, (c + 1) * LANES)
+            forced = dot(hot[pl.ds((2 * t + c) * rows, rows), :], values)
+            before = first_ref[level, :, part] if t == 0 and level < KEPT else second_ref[level if t == 1 else levels + level - KEPT, :, part]
+            total = before + forced
+            ends.append(total)
+            masked = total * ocean_ref[level, c].astype(F32)
+            state_ref[k, c] = masked
+            low[level, 3 * t : 3 * t + 3, part] = masked[0:3]
+            high[level, 3 * t : 3 * t + 3, part] = masked[rows - 3 : rows]
+        held = out_strip_ref[tile]
+        held = jnp.where(between(wide, first + 3, first + 9), turn(ends[0], first + 3), held)
+        out_strip_ref[tile] = jnp.where(
+            between(wide, first + 9, first + 15), turn(ends[1], first + 15), held
+        )
+
+    for t in range(2):
+        for level in range(levels):
+            if t == 0 and level == KEPT:
+                rest.wait()
+            if t == 1 and level % part == 0:
+                fetch[level // part].wait()
+            one(t, level)
     for tile in range(STRIPS):
         out_strip_ref[tile] = out_strip_ref[tile] * fields_ref[2, tile]
     for out, side in ((low, slice(0, 3)), (high, slice(rows - 3, rows))):
@@ -461,7 +475,7 @@
     swap_b_ref[...] = jnp.where(odd, high[...], low[...]).astype(BF16)
 
 
-def place_records(odd, arrived, adj, ocean, strip, fields, spread):
+def place_records(odd, arrived, first, adj, ocean, strip, fields, spread):
     levels, rows, cells = adj.shape[1:]
     devices = arrived.shape[0]
     edge = jax.ShapeDtypeStruct((levels + 1, 8, cells), BF16)
@@ -474,17 +488,17 @@
             edge,
             edge,
         ),
-        in_specs=[SMEM, VMEM, HBM] + [VMEM] * 4,
+        in_specs=[SMEM, VMEM, VMEM, HBM] + [VMEM] * 4,
         out_specs=(VMEM,) * 4,
         scratch_shapes=[
-            pltpu.VMEM(adj.shape, F32),
+            pltpu.VMEM((2 * levels - KEPT, rows, cells), F32),
             pltpu.VMEM((4 * rows, devices * 8), BF16),
             pltpu.VMEM(edge.shape, F32),
             pltpu.VMEM(edge.shape, F32),
-            pltpu.SemaphoreType.DMA((levels,)),
+            pltpu.SemaphoreType.DMA((3,)),
         ],
         compiler_params=pltpu.CompilerParams(vmem_limit_bytes=24 << 20),
-    )(odd, arrived, hbm(adj), ocean, strip, fields, spread)
+    )(odd, arrived, first, hbm(adj), ocean, strip, fields, spread)
 
 
 def steps_body(
@@ -520,19 +534,23 @@
 ):
     levels, rows = ocean_ref.shape[0], ocean_ref.shape[2]
 
-    def arrivals(level):
+    groups = ((0, 2), (2, levels))
+
+    def arrivals(group):
+        first, end = groups[group]
+        span = pl.ds(first, end - first)
         return [
             pltpu.make_async_copy(
-                source.at[level, :, pl.ds(x * LANES, LANES)],
-                flow_all.at[level, f, x, pl.ds(16, rows), :],
-                level_sems.at[2 * f + x, level],
+                source.at[span, :, pl.ds(x * LANES, LANES)],
+                flow_all.at[span, f, x, pl.ds(16, rows), :],
+                level_sems.at[2 * f + x, group],
             )
             for f, source in enumerate((ef_hbm, nf_hbm))
             for x in range(2)
         ]
 
-    for level in range(levels):
-        for copy in arrivals(level):
+    for group in range(2):
+        for copy in arrivals(group):
             copy.start()
     tall = rows + 16
     inner = slice(16, 16 + rows)
@@ -633,23 +651,25 @@
                     dest[0, 0, at] = total * strip_ocean[0, at]
             source = dest.at[0] if dest is not None else None
 
-    def copies(level, slot):
-        return [
-            pltpu.make_async_copy(done.at[slot, t], out_ref.at[t, level], sems.at[slot, t])
-            for t in range(2)
-        ]
+    def leave(level):
+        return pltpu.make_async_copy(done.at[:, level], out_ref.at[:, level], sems.at[level])
 
     def one(level, carry):
         flow = flow_all.at[level]
-        for copy in arrivals(level):
-            copy.wait()
+        for group in range(2):
+
+            @pl.when(level == groups[group][0])
+            def _():
+                for copy in arrivals(group):
+                    copy.wait()
+
         for f in range(2):
             for x in range(2):
                 flow[f, x, 0:16] = jnp.zeros((16, LANES), F32)
                 flow[f, x, 16 + rows : 32 + rows] = jnp.zeros((16, LANES), F32)
         for x in range(2):
             part = slice(x * LANES, (x + 1) * LANES)
-            ocean[x, inner] = ocean_ref[level, x]
+            ocean[x, inner] = ocean_ref[level, x].astype(F32)
             for f, dest in enumerate((flow.at[0, x], flow.at[1, x], ocean.at[x])):
                 dest[before] = rows_low[level, 3 * f : 3 * f + 3, part]
                 dest[after] = rows_high[level, 3 * f : 3 * f + 3, part]
@@ -665,13 +685,6 @@
             turned[1] = jnp.where(lane == 0, turned[0], turned[1])
             for x in range(2):
                 prepare(x, i, flow, faces[x], turned[x])
-        slot = lax.rem(level, 2)
-
-        @pl.when(level >= 2)
-        def _():
-            for copy in copies(level - 2, slot):
-                copy.wait()
-
         ks = [spread_ref[t, level] for t in range(2)]
         spots = [strip_of(t * levels + level) for t in range(2)]
         buffers = (cells_a, cells_b, cells_c)
@@ -693,17 +706,15 @@
                         tile, first = spots[t]
                         shift, keep = (125 - first, lane < 3) if x == 0 else (113 - first, lane >= 125)
                         fixed = turn(patch[tile, 8 * i - 16 : 8 * i - 8], shift)
-                        done[slot, t, 8 * i - 16 : 8 * i - 8, x * LANES : (x + 1) * LANES] = (
+                        done[t, level, 8 * i - 16 : 8 * i - 8, x * LANES : (x + 1) * LANES] = (
                             jnp.where(keep, fixed, total)
                         )
-        for copy in copies(level, slot):
-            copy.start()
+        leave(level).start()
         return carry
 
     lax.fori_loop(0, levels, one, 0)
-    for level in (levels - 2, levels - 1):
-        for copy in copies(level, level % 2):
-            copy.wait()
+    for level in range(levels):
+        leave(level).wait()
 
 
 def run_steps(where, spread, state, strip, swap_a, swap_b, ef, nf, ocean, fields, low, high):
@@ -730,9 +741,9 @@
             pltpu.VMEM(swap_a.shape, F32),
             pltpu.VMEM(low.shape, F32),
             pltpu.VMEM(low.shape, F32),
-            pltpu.VMEM((2, 2, rows, width), F32),
-            pltpu.SemaphoreType.DMA((2, 2)),
-            pltpu.SemaphoreType.DMA((4, levels)),
+            pltpu.VMEM((2, levels, rows, width), F32),
+            pltpu.SemaphoreType.DMA((levels,)),
+            pltpu.SemaphoreType.DMA((4, 2)),
         ],
         compiler_params=pltpu.CompilerParams(vmem_limit_bytes=24 << 20),
     )(where, spread, state, strip, swap_a, swap_b, hbm(ef), hbm(nf), ocean, fields, low, high)
@@ -770,21 +781,20 @@
     lat = lax.axis_index("lat")
     odd = lat % 2
     where = jnp.stack([lat == 0, lat == n_lat - 1, odd == 1]).astype(jnp.int32)
-    packed = pack_records(
-        forcing.transpose(0, 1, 3, 2, 4), obs_tile, obs_block, obs_live, n_lat * n_lon, n_lon
-    )
+    flat = forcing.transpose(0, 1, 3, 2, 4).reshape(-1, forcing.shape[4])
+    packed = pack_records(flat, obs_tile, obs_block, obs_live, n_lat * n_lon, n_lon)
     arrived = lax.all_to_all(packed, ("lat", "lon"), split_axis=0, concat_axis=0, tiled=True)
     columns, ocean = outer_columns(adjoint_in, east_flow, north_flow, land_mask)
     west = around(columns, "lon", 1)
     east = around(columns, "lon", -1)
-    own, spread = own_strips(east_flow, north_flow, ocean)
-    fields, adj_strip, low, high = outer_rows(
-        west, east, east_flow, north_flow, ocean, own, spread
+    own, spread, rest, adj_first, low, high = own_strips(
+        east_flow, north_flow, adjoint_in, ocean
     )
+    fields, adj_strip, low, high = outer_rows(west, east, own, spread, rest, low, high)
     below = along(high, "lat", 1)
     above = along(low, "lat", -1)
     state, strip, swap_a, swap_b = place_records(
-        odd.reshape(1).astype(jnp.int32), arrived, adjoint_in, ocean, adj_strip, fields, spread
+        odd.reshape(1).astype(jnp.int32), arrived, adj_first, adjoint_in, ocean, adj_strip, fields, spread
     )
     swap_a = swapped(swap_a, "lat", 0)
     swap_b = swapped(swap_b, "lat", 1)

time: 50.5 us -> 46.6 us (0.923)
  Pallas kernels: 27.8 us -> 23.5 us
  waiting for transfers between devices: 2.92 us -> 3.71 us
    pallas_call x1, Pallas kernels: 10.9 us -> 8.94 us  [run_steps(): pl.pallas_call(steps_body, name='three_steps', out_shape=jax.ShapeDtypeSt...]
    pallas_call x1, Pallas kernels: 3.99 us -> 2.68 us  [place_records(): pl.pallas_call(place_body, name='place_records', out_shape=(jax.ShapeDtyp...]
    pallas_call x1, Pallas kernels: 5.44 us -> 4.92 us  [own_strips(): pl.pallas_call(own_body, name='own_strips', out_shape=(jax.ShapeDtypeStru...]
    ppermute x2, waiting for transfers between devices: 0.95 us -> 1.47 us  [around(): lax.ppermute(block, axis, [(i, (i + distance) % count) for i in range(cou...]
  transfers between devices with their start and end apart: 7 -> 7, of which waited for: 2 -> 2; matrix products, arithmetic and copies ran while one was open for 0% -> 0% of each run, Pallas kernels for 29% -> 26%
where the time goes in v1:
time: 46.6 us; the launch traced here: 46.2 us
  Pallas kernels  23.5 us (50%)
  starting transfers between devices  18.2 us (39%)
  waiting for transfers between devices  3.71 us (8%)
  between operations  0.75 us (2%)
    pallas_call x1, Pallas kernels, run_steps(): pl.pallas_call(steps_body, name='three_steps', out_shape=jax.ShapeDtypeSt...  8.94 us
    all_to_all x1, starting transfers between devices, per_device(): lax.all_to_all(packed, ('lat', 'lon'), split_axis=0, concat_axis=0, tiled...  6.05 us
    ppermute x2, starting transfers between devices, along(): return lax.ppermute(block, axis, route)  5.83 us
    pallas_call x1, Pallas kernels, own_strips(): pl.pallas_call(own_body, name='own_strips', out_shape=(jax.ShapeDtypeStru...  4.92 us
    ppermute x2, starting transfers between devices, swapped(): lax.ppermute(block, axis, [(i, i + 1) for i in lower] + [(i + 1, i) for i...  4.1 us
    pallas_call x1, Pallas kernels, outer_columns(): pl.pallas_call(columns_body, name='outer_columns', out_shape=(jax.ShapeDt...  3.67 us
    pallas_call x1, Pallas kernels, place_records(): pl.pallas_call(place_body, name='place_records', out_shape=(jax.ShapeDtyp...  2.68 us
    pallas_call x1, Pallas kernels, pack_records(): pl.pallas_call(functools.partial(pack_body, n_lon), name='pack_records',...  2.36 us
  transfers between devices with their start and end apart: 7, of which 2 were waited for; matrix products, arithmetic and copies ran while one was open for 0% of the time, Pallas kernels for 26%

profile of v1, /device:TPU:8, one launch (start us, length us, event | category | flops | bytes accessed | tf_op | source)
XLA Modules:
  0.0 46.2 jit_solution(3260855702113343789)
XLA Ops:
  0.7 2.4 %pack_records.1 = bf16[32,11,8,128]{3,2,1,0:T(8,128)(2,1)} custom-call(s32[1]{0:T(128)S(6)} %copy.10.live_ref, s32[1,64]{1,0:T(1,128)} %tile_in.1, s32[1,64]{1,0:T(1,128)} %block_in.1, bf16[1280,128]{1,0:T(8,128)(2,1)} %bitcast.7), custom_call_target="tpu_custom_call" | custom-call | tf_op jit(solution)/shard_map/pack_records/pallas_call | solution.py:125
  3.0 6.0 %all-to-all-start = ((bf16[32,11,8,128]{3,2,1,0:T(8,128)(2,1)}), bf16[32,11,8,128]{3,2,1,0:T(8,128)(2,1)S(1)}, u32[]{:S(2)}, u32[]{:S(2)}) async-start(bf16[32,11,8,128]{3,2,1,0:T(8,128)(2,1)} %pack_records.1), calls=%async_computation | async-start | bytes 1441792 | tf_op jit(solution)/shard_map/all_to_all | solution.py:786
  9.1 3.7 %outer_columns.1 = (bf16[128,384]{1,0:T(8,128)(2,1)S(1)}, bf16[10,2,128,128]{3,2,1,0:T(8,128)(2,1)S(1)}) custom-call(f32[2,10,128,256]{3,2,1,0:T(8,128)} %adj_hbm.5, f32[10,128,256]{2,1,0:T(8,128)} %ef_hbm.5, f32[10,128,256]{2,1,0:T(8,128)} %nf_hbm.5, s32[10,128,256]{2,1,0:T(8,128)} %mask_hbm.1), custom_call_target="tpu_custom_call" | custom-call | tf_op jit(solution)/shard_map/outer_columns/pallas_call | solution.py:216
  12.7 2.2 %collective-permute-start.1 = (bf16[128,384]{1,0:T(8,128)(2,1)S(1)}, bf16[128,384]{1,0:T(8,128)(2,1)S(1)}, u32[]{:S(2)}, u32[]{:S(2)}) collective-permute-start(bf16[128,384]{1,0:T(8,128)(2,1)S(1)} %get-tuple-element.23), channel_id=1, source_target_pairs={{0,7},{1,0},{2,1},{3,2},{4,3},{5,4},{6,5},{7,6},{8,15},{9,8},{10,9... | collective-permute-start | bytes 294920 | tf_op jit(solution)/shard_map/ppermute | solution.py:754
  14.9 0.0 collective-permute-start
  14.9 4.9 %own_strips.1 = (f32[3,3,128,128]{3,2,1,0:T(8,128)S(1)}, bf16[128,384]{1,0:T(8,128)(2,1)S(1)}, bf16[2,128,384]{2,1,0:T(8,128)(2,1)S(1)}, f32[9,128,256]{2,1,0:T(...) custom-call(f32[10,128,256]{2,1,0:T(8,128)} %ef_hbm.5, f32[10,128,256]{2,1,0:T(8,128)} %nf_hbm.5, ...), custom_call_target="tpu_custom_call" | custom-call | flops 100000000 | bytes 10000000 | tf_op jit(solution)/shard_map/own_strips/pallas_call | solution.py:306
  19.9 0.0 collective-permute-done.1.east
  19.9 1.5 %collective-permute-done.west = bf16[128,384]{1,0:T(8,128)(2,1)S(1)} collective-permute-done((bf16[128,384]{1,0:T(8,128)(2,1)S(1)}, bf16[128,384]{1,0:T(8,128)(2,1)S(1)}, u32[]{:S(2)}, u32[]{:S(2)}) %collective-permute-start) | collective-permute-done | bytes 98336 | tf_op jit(solution)/shard_map/ppermute | solution.py:754
  21.3 0.9 %outer_rows.1 = (f32[3,3,128,128]{3,2,1,0:T(8,128)S(1)}, bf16[3,128,128]{2,1,0:T(8,128)(2,1)S(1)}, bf16[12,16,256]{2,1,0:T(8,128)(2,1)}, bf16[12,16,256]{2,1,0:T(8,128)(2,1)}) custom-call(bf16[128,384]{1,0:T(8,128)(2,1)S(1)} %collective-permute-done.west, bf16[128,384]{1,0:T(8,128)(2,1)S(1)} %collective-permute-done.1.east, ...), custom_call_target="tpu_custom_call" | custom-call | tf_op jit(solution)/shard_map/outer_rows/pallas_call | solution.py:366
  22.2 2.7 %collective-permute-start.4 = (bf16[12,16,256]{2,1,0:T(8,128)(2,1)}, bf16[12,16,256]{2,1,0:T(8,128)(2,1)S(1)}, u32[]{:S(2)}, u32[]{:S(2)}) collective-permute-start(bf16[12,16,256]{2,1,0:T(8,128)(2,1)} %get-tuple-element.35), channel_id=1, source_target_pairs={{0,8},{8,16},{16,24},{1,9},{9,17},{17,25},{2,10},{10,18},{18,26},{... | collective-permute-start | bytes 294920 | tf_op jit(solution)/shard_map/ppermute | solution.py:760
  25.0 3.1 %collective-permute-start.5 = (bf16[12,16,256]{2,1,0:T(8,128)(2,1)}, bf16[12,16,256]{2,1,0:T(8,128)(2,1)S(1)}, u32[]{:S(2)}, u32[]{:S(2)}) collective-permute-start(bf16[12,16,256]{2,1,0:T(8,128)(2,1)} %get-tuple-element.36), channel_id=1, source_target_pairs={{8,0},{16,8},{24,16},{9,1},{17,9},{25,17},{10,2},{18,10},{26,18},{... | collective-permute-start | bytes 294920 | tf_op jit(solution)/shard_map/ppermute | solution.py:760
  28.1 0.0 all-to-all-done.arrived_ref
  28.1 0.0 copy-start
  28.1 2.7 %place_records.1 = (f32[20,2,128,128]{3,2,1,0:T(8,128)S(1)}, f32[3,128,128]{2,1,0:T(8,128)S(1)}, bf16[11,8,256]{2,1,0:T(8,128)(2,1)S(1)}, bf16[11,8,256]{2,1,0:T(8,128)(2,1)S(1)}) custom-call(s32[1]{0:T(128)} %bitcast.3.odd_ref, bf16[32,11,8,128]{3,2,1,0:T(8,128)(2,1)S(1)} %all-to-all-done.arrived_ref, f32[9,128,256]{2,1,0:T(8,128)S(1)} %get-tuple-element.22.first_ref, ...), custom_call_target="tpu_custom_call" | custom-call | tf_op jit(solution)/shard_map/place_records/pallas_call | solution.py:482
  30.8 0.5 %collective-permute-start.2 = (bf16[11,8,256]{2,1,0:T(8,128)(2,1)S(1)}, bf16[11,8,256]{2,1,0:T(8,128)(2,1)S(1)}, u32[]{:S(2)}, u32[]{:S(2)}) collective-permute-start(bf16[11,8,256]{2,1,0:T(8,128)(2,1)S(1)} %get-tuple-element.33), channel_id=1, source_target_pairs={{0,8},{16,24},{8,0},{24,16},{1,9},{17,25},{9,1},{25,17},{2,10},{18... | collective-permute-start | bytes 135176 | tf_op jit(solution)/shard_map/ppermute | solution.py:766
  31.3 3.6 %collective-permute-start.3 = (bf16[11,8,256]{2,1,0:T(8,128)(2,1)S(1)}, bf16[11,8,256]{2,1,0:T(8,128)(2,1)S(1)}, u32[]{:S(2)}, u32[]{:S(2)}) collective-permute-start(bf16[11,8,256]{2,1,0:T(8,128)(2,1)S(1)} %get-tuple-element.34), channel_id=1, source_target_pairs={{8,16},{16,8},{9,17},{17,9},{10,18},{18,10},{11,19},{19,11},{12,20... | collective-permute-start | bytes 135176 | tf_op jit(solution)/shard_map/ppermute | solution.py:766
  34.9 0.1 add_convert_fusion.where_ref
  35.0 0.0 collective-permute-done.4.low_ref
  35.0 0.0 collective-permute-done.5.high_ref
  35.0 0.0 collective-permute-done.2.swap_a_ref
  35.0 2.2 %collective-permute-done.3.swap_b_ref = bf16[11,8,256]{2,1,0:T(8,128)(2,1)S(1)} collective-permute-done((bf16[11,8,256]{2,1,0:T(8,128)(2,1)S(1)}, bf16[11,8,256]{2,1,0:T(8,128)(2,1)S(1)}, u32[]{:S(2)}, u32[]{:S(2)}) %collective-permute-start.3) | collective-permute-done | bytes 45088 | tf_op jit(solution)/shard_map/ppermute | solution.py:766
  37.2 0.0 copy-done
  37.2 8.9 %three_steps.1 = f32[2,10,128,256]{3,2,1,0:T(8,128)} custom-call(s32[3]{0:T(128)S(1)} %add_convert_fusion.where_ref, f32[2,10]{1,0:T(2,128)S(1)} %copy-done, f32[20,2,128,128]{3,2,1,0:T(8,128)S(1)} %get-tuple-element.31.state_ref, f32[3,128,128]{2,1,0:T(8,128)S(1)} %get-tuple-element.32.strip_ref, bf16[11,8,256]{2,1,0:T(8,128)(2,1)S(1)} %collective-permute-done.2.swap_a_ref, ...), custom_call_target="tpu_custom_call" | custom-call | tf_op jit(solution)/shard_map/three_steps/pallas_call | solution.py:724
Async XLA Ops:
  3.0 25.1 %all-to-all-start = ((bf16[32,11,8,128]{3,2,1,0:T(8,128)(2,1)}), bf16[32,11,8,128]{3,2,1,0:T(8,128)(2,1)S(1)}, u32[]{:S(2)}, u32[]{:S(2)}) async-start(bf16[32,11,8,128]{3,2,1,0:T(8,128)(2,1)} %pack_records.1), calls=%async_computation | async-start | bytes 1441792 | tf_op jit(solution)/shard_map/all_to_all | solution.py:786
  12.7 7.1 %collective-permute-start.1 = (bf16[128,384]{1,0:T(8,128)(2,1)S(1)}, bf16[128,384]{1,0:T(8,128)(2,1)S(1)}, u32[]{:S(2)}, u32[]{:S(2)}) collective-permute-start(bf16[128,384]{1,0:T(8,128)(2,1)S(1)} %get-tuple-element.23), channel_id=1, source_target_pairs={{0,7},{1,0},{2,1},{3,2},{4,3},{5,4},{6,5},{7,6},{8,15},{9,8},{10,9... | collective-permute-start | bytes 294920 | tf_op jit(solution)/shard_map/ppermute | solution.py:754
  14.9 6.4 %collective-permute-start = (bf16[128,384]{1,0:T(8,128)(2,1)S(1)}, bf16[128,384]{1,0:T(8,128)(2,1)S(1)}, u32[]{:S(2)}, u32[]{:S(2)}) collective-permute-start(bf16[128,384]{1,0:T(8,128)(2,1)S(1)} %get-tuple-element.23), channel_id=1, source_target_pairs={{0,1},{1,2},{2,3},{3,4},{4,5},{5,6},{6,7},{7,0},{8,9},{9,10},{10,1... | collective-permute-start | bytes 294920 | tf_op jit(solution)/shard_map/ppermute | solution.py:754
  22.2 12.7 %collective-permute-start.4 = (bf16[12,16,256]{2,1,0:T(8,128)(2,1)}, bf16[12,16,256]{2,1,0:T(8,128)(2,1)S(1)}, u32[]{:S(2)}, u32[]{:S(2)}) collective-permute-start(bf16[12,16,256]{2,1,0:T(8,128)(2,1)} %get-tuple-element.35), channel_id=1, source_target_pairs={{0,8},{8,16},{16,24},{1,9},{9,17},{17,25},{2,10},{10,18},{18,26},{... | collective-permute-start | bytes 294920 | tf_op jit(solution)/shard_map/ppermute | solution.py:760
  25.0 10.0 %collective-permute-start.5 = (bf16[12,16,256]{2,1,0:T(8,128)(2,1)}, bf16[12,16,256]{2,1,0:T(8,128)(2,1)S(1)}, u32[]{:S(2)}, u32[]{:S(2)}) collective-permute-start(bf16[12,16,256]{2,1,0:T(8,128)(2,1)} %get-tuple-element.36), channel_id=1, source_target_pairs={{8,0},{16,8},{24,16},{9,1},{17,9},{25,17},{10,2},{18,10},{26,18},{... | collective-permute-start | bytes 294920 | tf_op jit(solution)/shard_map/ppermute | solution.py:760
  28.1 9.1 %copy-start = (f32[2,10]{1,0:T(2,128)S(1)}, f32[2,10]{1,0:T(2,128)}, u32[]{:S(2)}) copy-start(f32[2,10]{1,0:T(2,128)} %spread_ref.1) | copy-start | bytes 244
  30.8 4.2 %collective-permute-start.2 = (bf16[11,8,256]{2,1,0:T(8,128)(2,1)S(1)}, bf16[11,8,256]{2,1,0:T(8,128)(2,1)S(1)}, u32[]{:S(2)}, u32[]{:S(2)}) collective-permute-start(bf16[11,8,256]{2,1,0:T(8,128)(2,1)S(1)} %get-tuple-element.33), channel_id=1, source_target_pairs={{0,8},{16,24},{8,0},{24,16},{1,9},{17,25},{9,1},{25,17},{2,10},{18... | collective-permute-start | bytes 135176 | tf_op jit(solution)/shard_map/ppermute | solution.py:766
  31.3 5.9 %collective-permute-start.3 = (bf16[11,8,256]{2,1,0:T(8,128)(2,1)S(1)}, bf16[11,8,256]{2,1,0:T(8,128)(2,1)S(1)}, u32[]{:S(2)}, u32[]{:S(2)}) collective-permute-start(bf16[11,8,256]{2,1,0:T(8,128)(2,1)S(1)} %get-tuple-element.34), channel_id=1, source_target_pairs={{8,16},{16,8},{9,17},{17,9},{10,18},{18,10},{11,19},{19,11},{12,20... | collective-permute-start | bytes 135176 | tf_op jit(solution)/shard_map/ppermute | solution.py:766

commit v2 on v1

--- a/solution.py
+++ b/solution.py
@@ -74,34 +74,33 @@
     east = band + jnp.where(column == n_lon - 1, 0.0, column + 1.0)
     west = band + jnp.where(column == 0.0, n_lon - 1.0, column - 1.0)
     half = block - 2.0 * jnp.floor(block * 0.5)
-    code = jnp.where(live, tile * 8.0 + rank, -8.0)
-    to_east = jnp.where(live & (half == 1.0), east * 8.0 + rank, -8.0)
-    to_west = jnp.where(live & (half == 0.0), west * 8.0 + rank, -8.0)
+    code = jnp.where(live, tile * 4.0 + rank, -8.0)
+    to_east = jnp.where(live & (half == 1.0), east * 4.0 + rank, -8.0)
+    to_west = jnp.where(live & (half == 0.0), west * 4.0 + rank, -8.0)
     moves[2].wait()
     wide[...] = forcing_ref[...].astype(F32)
     sent = []
 
     def send(q, values):
-        out_ref[:, q] = values.astype(BF16).reshape(devices, 8, LANES)
-        copy = pltpu.make_async_copy(out_ref.at[:, q], out_hbm.at[:, q], out_sems.at[q])
-        copy.start()
-        sent.append(copy)
-
-    first, second = one_hot(devices * 8, code), one_hot(devices * 8, code + 4.0)
+        out_ref[:, q] = values.astype(BF16).reshape(devices, 4, LANES)
+        if q % 2 == 1 or q == count:
+            span = pl.ds(q, 1) if q == count else pl.ds(q - 1, 2)
+            copy = pltpu.make_async_copy(
+                out_ref.at[:, span], out_hbm.at[:, span], out_sems.at[q // 2]
+            )
+            copy.start()
+            sent.append(copy)
+
+    first = one_hot(devices * 4, code)
     lane = iota((records, LANES), 1)
     edges = jnp.zeros((records, LANES), F32)
-    pair = []
     for place in range(count):
         level, t = divmod(place, 2)
         k = t * levels + level
         values = wide[pl.ds(place, records, stride=count), :]
         turned = pltpu.roll(values, (6 * k + 3) % LANES, 1)
         edges = jnp.where((lane >= 6 * k) & (lane < 6 * k + 6), turned, edges)
-        pair.append(values.astype(BF16))
-        if t == 1:
-            packed = dot(first, pair[0]) + dot(second, pair[1])
-            send(level, packed)
-            pair = []
+        send(place, dot(first, values.astype(BF16)))
     row_col = jnp.floor(block_col * 0.5) + 1.0
     mine = west_lane((records, LANES))
     data = lane < 6 * count
@@ -110,10 +109,10 @@
     header = jnp.where(lane == 120, block_col + 1.0, 0.0)
     last = (
         dot(first, header.astype(BF16))
-        + dot(one_hot(devices * 8, to_east), from_west.astype(BF16))
-        + dot(one_hot(devices * 8, to_west), from_east.astype(BF16))
+        + dot(one_hot(devices * 4, to_east), from_west.astype(BF16))
+        + dot(one_hot(devices * 4, to_west), from_east.astype(BF16))
     )
-    send(count // 2, last)
+    send(count, last)
     for copy in sent:
         copy.wait()
 
@@ -121,7 +120,7 @@
 def pack_records(forcing, tile, block, live, devices, n_lon):
     records, width = tile.shape[1], forcing.shape[1]
     levels = forcing.shape[0] // records // 2
-    out = (devices, levels + 1, 8, width)
+    out = (devices, 2 * levels + 1, 4, width)
     return pl.pallas_call(
         functools.partial(pack_body, n_lon),
         name="pack_records",
@@ -399,7 +398,7 @@
     sems,
 ):
     devices = arrived_ref.shape[0]
-    slots = devices * 8
+    slots = devices * 4
     levels, rows = ocean_ref.shape[0], first_ref.shape[1]
     part = levels // 2
     late = levels - KEPT
@@ -414,14 +413,12 @@
     )
     for copy in [rest] + fetch:
         copy.start()
-    last = arrived_ref[:, levels].astype(F32).reshape(slots, LANES)
+    last = arrived_ref[:, 2 * levels].astype(F32).reshape(slots, LANES)
     heads = last.T[120:128]
-    later = pltpu.roll(heads, 4, 1)
     row = fiota((rows, slots), 0)
-    for b, source in enumerate((heads, later)):
-        for c in range(2):
-            found = source[0:1] == 2.0 * row + (c + 1.0)
-            hot[pl.ds((2 * b + c) * rows, rows), :] = jnp.where(found, 1.0, 0.0).astype(BF16)
+    for c in range(2):
+        found = heads[0:1] == 2.0 * row + (c + 1.0)
+        hot[pl.ds(c * rows, rows), :] = jnp.where(found, 1.0, 0.0).astype(BF16)
     lane = iota((slots, LANES), 1)
     mine = west_lane((slots, LANES))
     from_west = jnp.where(mine & (lane < 120), last, 0.0).astype(BF16)
@@ -437,13 +434,13 @@
     wide = iota((rows, LANES), 1)
 
     def one(t, level):
-        values = arrived_ref[:, level].astype(F32).reshape(slots, LANES).astype(BF16)
+        values = arrived_ref[:, 2 * level + t].astype(F32).reshape(slots, LANES).astype(BF16)
         k = t * levels + level
         tile, first = strip_of(k)
         ends = []
         for c in range(2):
             part = slice(c * LANES, (c + 1) * LANES)
-            forced = dot(hot[pl.ds((2 * t + c) * rows, rows), :], values)
+            forced = dot(hot[pl.ds(c * rows, rows), :], values)
             before = first_ref[level, :, part] if t == 0 and level < KEPT else second_ref[level if t == 1 else levels + level - KEPT, :, part]
             total = before + forced
             ends.append(total)
@@ -492,7 +489,7 @@
         out_specs=(VMEM,) * 4,
         scratch_shapes=[
             pltpu.VMEM((2 * levels - KEPT, rows, cells), F32),
-            pltpu.VMEM((4 * rows, devices * 8), BF16),
+            pltpu.VMEM((2 * rows, devices * 4), BF16),
             pltpu.VMEM(edge.shape, F32),
             pltpu.VMEM(edge.shape, F32),
             pltpu.SemaphoreType.DMA((3,)),

time: 46.6 us -> 46.3 us (level)
  waiting for transfers between devices: 3.71 us -> 3.14 us
  transfers between devices with their start and end apart: 7 -> 7, of which waited for: 2 -> 2; matrix products, arithmetic and copies ran while one was open for 0% -> 0% of each run, Pallas kernels for 26% -> 27%
where the time goes in v2:
time: 46.3 us; the launch traced here: 45.6 us
  Pallas kernels  23.3 us (50%)
  starting transfers between devices  18.3 us (40%)
  waiting for transfers between devices  3.14 us (7%)
  between operations  0.76 us (2%)
    pallas_call x1, Pallas kernels, run_steps(): pl.pallas_call(steps_body, name='three_steps', out_shape=jax.ShapeDtypeSt...  8.94 us
    all_to_all x1, starting transfers between devices, per_device(): lax.all_to_all(packed, ('lat', 'lon'), split_axis=0, concat_axis=0, tiled...  6.05 us
    ppermute x2, starting transfers between devices, along(): return lax.ppermute(block, axis, route)  5.83 us
    pallas_call x1, Pallas kernels, own_strips(): pl.pallas_call(own_body, name='own_strips', out_shape=(jax.ShapeDtypeStru...  4.92 us
    ppermute x2, starting transfers between devices, swapped(): lax.ppermute(block, axis, [(i, i + 1) for i in lower] + [(i + 1, i) for i...  4.2 us
    pallas_call x1, Pallas kernels, outer_columns(): pl.pallas_call(columns_body, name='outer_columns', out_shape=(jax.ShapeDt...  3.67 us
    pallas_call x1, Pallas kernels, place_records(): pl.pallas_call(place_body, name='place_records', out_shape=(jax.ShapeDtyp...  2.67 us
    pallas_call x1, Pallas kernels, pack_records(): pl.pallas_call(functools.partial(pack_body, n_lon), name='pack_records',...  2.22 us
  transfers between devices with their start and end apart: 7, of which 2 were waited for; matrix products, arithmetic and copies ran while one was open for 0% of the time, Pallas kernels for 27%

profile of v2, /device:TPU:8, one launch (start us, length us, event | category | flops | bytes accessed | tf_op | source)
XLA Modules:
  0.0 45.6 jit_solution(4076490456669098335)
XLA Ops:
  0.7 2.2 %pack_records.1 = bf16[32,21,4,128]{3,2,1,0:T(4,128)(2,1)} custom-call(s32[1]{0:T(128)S(6)} %copy.10.live_ref, s32[1,64]{1,0:T(1,128)} %tile_in.1, s32[1,64]{1,0:T(1,128)} %block_in.1, bf16[1280,128]{1,0:T(8,128)(2,1)} %bitcast.7), custom_call_target="tpu_custom_call" | custom-call | tf_op jit(solution)/shard_map/pack_records/pallas_call | solution.py:124
  2.9 6.0 %all-to-all-start = ((bf16[32,21,4,128]{3,2,1,0:T(4,128)(2,1)}), bf16[32,21,4,128]{3,2,1,0:T(4,128)(2,1)S(1)}, u32[]{:S(2)}, u32[]{:S(2)}) async-start(bf16[32,21,4,128]{3,2,1,0:T(4,128)(2,1)} %pack_records.1), calls=%async_computation | async-start | bytes 1376256 | tf_op jit(solution)/shard_map/all_to_all | solution.py:783
  8.9 3.7 %outer_columns.1 = (bf16[128,384]{1,0:T(8,128)(2,1)S(1)}, bf16[10,2,128,128]{3,2,1,0:T(8,128)(2,1)S(1)}) custom-call(f32[2,10,128,256]{3,2,1,0:T(8,128)} %adj_hbm.5, f32[10,128,256]{2,1,0:T(8,128)} %ef_hbm.5, f32[10,128,256]{2,1,0:T(8,128)} %nf_hbm.5, s32[10,128,256]{2,1,0:T(8,128)} %mask_hbm.1), custom_call_target="tpu_custom_call" | custom-call | tf_op jit(solution)/shard_map/outer_columns/pallas_call | solution.py:215
  12.6 2.2 %collective-permute-start.1 = (bf16[128,384]{1,0:T(8,128)(2,1)S(1)}, bf16[128,384]{1,0:T(8,128)(2,1)S(1)}, u32[]{:S(2)}, u32[]{:S(2)}) collective-permute-start(bf16[128,384]{1,0:T(8,128)(2,1)S(1)} %get-tuple-element.23), channel_id=1, source_target_pairs={{0,7},{1,0},{2,1},{3,2},{4,3},{5,4},{6,5},{7,6},{8,15},{9,8},{10,9... | collective-permute-start | bytes 294920 | tf_op jit(solution)/shard_map/ppermute | solution.py:751
  14.8 0.0 collective-permute-start
  14.8 4.9 %own_strips.1 = (f32[3,3,128,128]{3,2,1,0:T(8,128)S(1)}, bf16[128,384]{1,0:T(8,128)(2,1)S(1)}, bf16[2,128,384]{2,1,0:T(8,128)(2,1)S(1)}, f32[9,128,256]{2,1,0:T(...) custom-call(f32[10,128,256]{2,1,0:T(8,128)} %ef_hbm.5, f32[10,128,256]{2,1,0:T(8,128)} %nf_hbm.5, ...), custom_call_target="tpu_custom_call" | custom-call | flops 100000000 | bytes 10000000 | tf_op jit(solution)/shard_map/own_strips/pallas_call | solution.py:305
  19.7 0.0 collective-permute-done.1.east
  19.7 1.2 %collective-permute-done.west = bf16[128,384]{1,0:T(8,128)(2,1)S(1)} collective-permute-done((bf16[128,384]{1,0:T(8,128)(2,1)S(1)}, bf16[128,384]{1,0:T(8,128)(2,1)S(1)}, u32[]{:S(2)}, u32[]{:S(2)}) %collective-permute-start) | collective-permute-done | bytes 98336 | tf_op jit(solution)/shard_map/ppermute | solution.py:751
  20.9 0.9 %outer_rows.1 = (f32[3,3,128,128]{3,2,1,0:T(8,128)S(1)}, bf16[3,128,128]{2,1,0:T(8,128)(2,1)S(1)}, bf16[12,16,256]{2,1,0:T(8,128)(2,1)}, bf16[12,16,256]{2,1,0:T(8,128)(2,1)}) custom-call(bf16[128,384]{1,0:T(8,128)(2,1)S(1)} %collective-permute-done.west, bf16[128,384]{1,0:T(8,128)(2,1)S(1)} %collective-permute-done.1.east, ...), custom_call_target="tpu_custom_call" | custom-call | tf_op jit(solution)/shard_map/outer_rows/pallas_call | solution.py:365
  21.8 3.1 %collective-permute-start.4 = (bf16[12,16,256]{2,1,0:T(8,128)(2,1)}, bf16[12,16,256]{2,1,0:T(8,128)(2,1)S(1)}, u32[]{:S(2)}, u32[]{:S(2)}) collective-permute-start(bf16[12,16,256]{2,1,0:T(8,128)(2,1)} %get-tuple-element.35), channel_id=1, source_target_pairs={{0,8},{8,16},{16,24},{1,9},{9,17},{17,25},{2,10},{10,18},{18,26},{... | collective-permute-start | bytes 294920 | tf_op jit(solution)/shard_map/ppermute | solution.py:757
  24.9 2.8 %collective-permute-start.5 = (bf16[12,16,256]{2,1,0:T(8,128)(2,1)}, bf16[12,16,256]{2,1,0:T(8,128)(2,1)S(1)}, u32[]{:S(2)}, u32[]{:S(2)}) collective-permute-start(bf16[12,16,256]{2,1,0:T(8,128)(2,1)} %get-tuple-element.36), channel_id=1, source_target_pairs={{8,0},{16,8},{24,16},{9,1},{17,9},{25,17},{10,2},{18,10},{26,18},{... | collective-permute-start | bytes 294920 | tf_op jit(solution)/shard_map/ppermute | solution.py:757
  27.7 0.0 all-to-all-done.arrived_ref
  27.7 0.0 copy-start
  27.7 2.7 %place_records.1 = (f32[20,2,128,128]{3,2,1,0:T(8,128)S(1)}, f32[3,128,128]{2,1,0:T(8,128)S(1)}, bf16[11,8,256]{2,1,0:T(8,128)(2,1)S(1)}, bf16[11,8,256]{2,1,0:T(8,128)(2,1)S(1)}) custom-call(s32[1]{0:T(128)} %bitcast.3.odd_ref, bf16[32,21,4,128]{3,2,1,0:T(4,128)(2,1)S(1)} %all-to-all-done.arrived_ref, f32[9,128,256]{2,1,0:T(8,128)S(1)} %get-tuple-element.22.first_ref, ...), custom_call_target="tpu_custom_call" | custom-call | tf_op jit(solution)/shard_map/place_records/pallas_call | solution.py:479
  30.4 0.1 collective-permute-start.2
  30.5 4.1 %collective-permute-start.3 = (bf16[11,8,256]{2,1,0:T(8,128)(2,1)S(1)}, bf16[11,8,256]{2,1,0:T(8,128)(2,1)S(1)}, u32[]{:S(2)}, u32[]{:S(2)}) collective-permute-start(bf16[11,8,256]{2,1,0:T(8,128)(2,1)S(1)} %get-tuple-element.34), channel_id=1, source_target_pairs={{8,16},{16,8},{9,17},{17,9},{10,18},{18,10},{11,19},{19,11},{12,20... | collective-permute-start | bytes 135176 | tf_op jit(solution)/shard_map/ppermute | solution.py:763
  34.6 0.1 add_convert_fusion.where_ref
  34.7 0.0 collective-permute-done.4.low_ref
  34.7 0.0 collective-permute-done.5.high_ref
  34.7 0.0 collective-permute-done.2.swap_a_ref
  34.7 1.9 %collective-permute-done.3.swap_b_ref = bf16[11,8,256]{2,1,0:T(8,128)(2,1)S(1)} collective-permute-done((bf16[11,8,256]{2,1,0:T(8,128)(2,1)S(1)}, bf16[11,8,256]{2,1,0:T(8,128)(2,1)S(1)}, u32[]{:S(2)}, u32[]{:S(2)}) %collective-permute-start.3) | collective-permute-done | bytes 45088 | tf_op jit(solution)/shard_map/ppermute | solution.py:763
  36.6 0.0 copy-done
  36.6 8.9 %three_steps.1 = f32[2,10,128,256]{3,2,1,0:T(8,128)} custom-call(s32[3]{0:T(128)S(1)} %add_convert_fusion.where_ref, f32[2,10]{1,0:T(2,128)S(1)} %copy-done, f32[20,2,128,128]{3,2,1,0:T(8,128)S(1)} %get-tuple-element.31.state_ref, f32[3,128,128]{2,1,0:T(8,128)S(1)} %get-tuple-element.32.strip_ref, bf16[11,8,256]{2,1,0:T(8,128)(2,1)S(1)} %collective-permute-done.2.swap_a_ref, ...), custom_call_target="tpu_custom_call" | custom-call | tf_op jit(solution)/shard_map/three_steps/pallas_call | solution.py:721
Async XLA Ops:
  2.9 24.8 %all-to-all-start = ((bf16[32,21,4,128]{3,2,1,0:T(4,128)(2,1)}), bf16[32,21,4,128]{3,2,1,0:T(4,128)(2,1)S(1)}, u32[]{:S(2)}, u32[]{:S(2)}) async-start(bf16[32,21,4,128]{3,2,1,0:T(4,128)(2,1)} %pack_records.1), calls=%async_computation | async-start | bytes 1376256 | tf_op jit(solution)/shard_map/all_to_all | solution.py:783
  12.6 7.1 %collective-permute-start.1 = (bf16[128,384]{1,0:T(8,128)(2,1)S(1)}, bf16[128,384]{1,0:T(8,128)(2,1)S(1)}, u32[]{:S(2)}, u32[]{:S(2)}) collective-permute-start(bf16[128,384]{1,0:T(8,128)(2,1)S(1)} %get-tuple-element.23), channel_id=1, source_target_pairs={{0,7},{1,0},{2,1},{3,2},{4,3},{5,4},{6,5},{7,6},{8,15},{9,8},{10,9... | collective-permute-start | bytes 294920 | tf_op jit(solution)/shard_map/ppermute | solution.py:751
  14.8 6.1 %collective-permute-start = (bf16[128,384]{1,0:T(8,128)(2,1)S(1)}, bf16[128,384]{1,0:T(8,128)(2,1)S(1)}, u32[]{:S(2)}, u32[]{:S(2)}) collective-permute-start(bf16[128,384]{1,0:T(8,128)(2,1)S(1)} %get-tuple-element.23), channel_id=1, source_target_pairs={{0,1},{1,2},{2,3},{3,4},{4,5},{5,6},{6,7},{7,0},{8,9},{9,10},{10,1... | collective-permute-start | bytes 294920 | tf_op jit(solution)/shard_map/ppermute | solution.py:751
  21.8 12.8 %collective-permute-start.4 = (bf16[12,16,256]{2,1,0:T(8,128)(2,1)}, bf16[12,16,256]{2,1,0:T(8,128)(2,1)S(1)}, u32[]{:S(2)}, u32[]{:S(2)}) collective-permute-start(bf16[12,16,256]{2,1,0:T(8,128)(2,1)} %get-tuple-element.35), channel_id=1, source_target_pairs={{0,8},{8,16},{16,24},{1,9},{9,17},{17,25},{2,10},{10,18},{18,26},{... | collective-permute-start | bytes 294920 | tf_op jit(solution)/shard_map/ppermute | solution.py:757
  24.9 9.8 %collective-permute-start.5 = (bf16[12,16,256]{2,1,0:T(8,128)(2,1)}, bf16[12,16,256]{2,1,0:T(8,128)(2,1)S(1)}, u32[]{:S(2)}, u32[]{:S(2)}) collective-permute-start(bf16[12,16,256]{2,1,0:T(8,128)(2,1)} %get-tuple-element.36), channel_id=1, source_target_pairs={{8,0},{16,8},{24,16},{9,1},{17,9},{25,17},{10,2},{18,10},{26,18},{... | collective-permute-start | bytes 294920 | tf_op jit(solution)/shard_map/ppermute | solution.py:757
  27.7 8.9 %copy-start = (f32[2,10]{1,0:T(2,128)S(1)}, f32[2,10]{1,0:T(2,128)}, u32[]{:S(2)}) copy-start(f32[2,10]{1,0:T(2,128)} %spread_ref.1) | copy-start | bytes 244
  30.4 4.3 %collective-permute-start.2 = (bf16[11,8,256]{2,1,0:T(8,128)(2,1)S(1)}, bf16[11,8,256]{2,1,0:T(8,128)(2,1)S(1)}, u32[]{:S(2)}, u32[]{:S(2)}) collective-permute-start(bf16[11,8,256]{2,1,0:T(8,128)(2,1)S(1)} %get-tuple-element.33), channel_id=1, source_target_pairs={{0,8},{16,24},{8,0},{24,16},{1,9},{17,25},{9,1},{25,17},{2,10},{18... | collective-permute-start | bytes 135176 | tf_op jit(solution)/shard_map/ppermute | solution.py:763
  30.5 6.2 %collective-permute-start.3 = (bf16[11,8,256]{2,1,0:T(8,128)(2,1)S(1)}, bf16[11,8,256]{2,1,0:T(8,128)(2,1)S(1)}, u32[]{:S(2)}, u32[]{:S(2)}) collective-permute-start(bf16[11,8,256]{2,1,0:T(8,128)(2,1)S(1)} %get-tuple-element.34), channel_id=1, source_target_pairs={{8,16},{16,8},{9,17},{17,9},{10,18},{18,10},{11,19},{19,11},{12,20... | collective-permute-start | bytes 135176 | tf_op jit(solution)/shard_map/ppermute | solution.py:763

commit v3 on v2

--- a/solution.py
+++ b/solution.py
@@ -328,8 +328,8 @@
 
 
 def edges_body(
-    west, east, own_ref, spread_ref, rest_ref, low_main, high_main,
-    strips, adj, low_out, high_out, held,
+    odd_ref, west, east, own_ref, spread_ref, rest_ref, low_main, high_main,
+    strips, adj, swap_a, swap_b, held,
 ):
     levels, rows = low_main.shape[0], own_ref.shape[2]
 
@@ -347,20 +347,22 @@
     for tile in range(STRIPS):
         adj[tile] = halos[:, tile * LANES : (tile + 1) * LANES].astype(BF16)
     held[...] = jnp.zeros_like(held)
-    for side, (out, main, first) in enumerate(
-        ((low_out, low_main, 0), (high_out, high_main, rows - 3))
-    ):
+    for side, first in enumerate((0, rows - 3)):
         at = slice(first, first + 3)
         for f in range(3):
             here = slice(3 * f, 3 * f + 3)
             held[side, 0, here, :LANES] = strips[f, 0, at, :]
             held[side, 0, here, LANES:] = strips[f, 1, at, :]
             held[side, 1, here, :LANES] = strips[f, 2, at, :]
-        out[0:levels] = main[...]
-        out[levels : levels + 2] = held[side].astype(BF16)
-
-
-def outer_rows(west, east, own, spread, rest, low, high):
+    odd = odd_ref[0] == 1
+    low, high = low_main[...].astype(F32), high_main[...].astype(F32)
+    swap_a[0:levels] = jnp.where(odd, low, high).astype(BF16)
+    swap_b[0:levels] = jnp.where(odd, high, low).astype(BF16)
+    swap_a[levels : levels + 2] = jnp.where(odd, held[0], held[1]).astype(BF16)
+    swap_b[levels : levels + 2] = jnp.where(odd, held[1], held[0]).astype(BF16)
+
+
+def outer_rows(odd, west, east, own, spread, rest, low, high):
     edge = (low.shape[0] + 2,) + low.shape[1:]
     return pl.pallas_call(
         edges_body,
@@ -371,11 +373,11 @@
             jax.ShapeDtypeStruct(edge, BF16),
             jax.ShapeDtypeStruct(edge, BF16),
         ),
-        in_specs=[VMEM] * 7,
+        in_specs=[SMEM] + [VMEM] * 7,
         out_specs=(VMEM,) * 4,
         scratch_shapes=[pltpu.VMEM((2, 2) + low.shape[1:], F32)],
         compiler_params=pltpu.CompilerParams(vmem_limit_bytes=24 << 20),
-    )(west, east, own, spread, rest, low, high)
+    )(odd, west, east, own, spread, rest, low, high)
 
 
 def place_body(
@@ -567,8 +569,9 @@
                 ref[t, x, 16 + rows : 32 + rows] = jnp.zeros((16, LANES), F32)
     below[...] = jnp.where(odd, swap_a_ref[...].astype(F32), swap_b_ref[...].astype(F32))
     above[...] = jnp.where(odd, swap_b_ref[...].astype(F32), swap_a_ref[...].astype(F32))
-    rows_low[...] = low_ref[...].astype(F32)
-    rows_high[...] = high_ref[...].astype(F32)
+    edge_a, edge_b = low_ref[...].astype(F32), high_ref[...].astype(F32)
+    rows_low[...] = jnp.where(odd, edge_a, edge_b)
+    rows_high[...] = jnp.where(odd, edge_b, edge_a)
     top = 8 + rows
     shut_s = (sub == 0) & (at_start == 1)
     shut_n = (sub == 7) & (at_end == 1)
@@ -751,12 +754,6 @@
     return lax.ppermute(block, axis, [(i, (i + distance) % count) for i in range(count)])
 
 
-def along(block, axis, distance):
-    count = lax.axis_size(axis)
-    route = [(i, i + distance) for i in range(count) if 0 <= i + distance < count]
-    return lax.ppermute(block, axis, route)
-
-
 def swapped(block, axis, start):
     count = lax.axis_size(axis)
     lower = range(start, count - 1, 2)
@@ -787,11 +784,14 @@
     own, spread, rest, adj_first, low, high = own_strips(
         east_flow, north_flow, adjoint_in, ocean
     )
-    fields, adj_strip, low, high = outer_rows(west, east, own, spread, rest, low, high)
-    below = along(high, "lat", 1)
-    above = along(low, "lat", -1)
+    parity = odd.reshape(1).astype(jnp.int32)
+    fields, adj_strip, edge_a, edge_b = outer_rows(
+        parity, west, east, own, spread, rest, low, high
+    )
+    edge_a = swapped(edge_a, "lat", 0)
+    edge_b = swapped(edge_b, "lat", 1)
     state, strip, swap_a, swap_b = place_records(
-        odd.reshape(1).astype(jnp.int32), arrived, adj_first, adjoint_in, ocean, adj_strip, fields, spread
+        parity, arrived, adj_first, adjoint_in, ocean, adj_strip, fields, spread
     )
     swap_a = swapped(swap_a, "lat", 0)
     swap_b = swapped(swap_b, "lat", 1)
@@ -806,8 +806,8 @@
         north_flow,
         ocean,
         fields,
-        below,
-        above,
+        edge_a,
+        edge_b,
     )
 
 

time: 46.3 us -> 45.7 us (0.987)
  starting transfers between devices: 18.3 us -> 15.3 us
  waiting for transfers between devices: 3.14 us -> 5.88 us
    ppermute x2 -> x0, starting transfers between devices: 5.83 us -> none  [along(): return lax.ppermute(block, axis, route)]
    ppermute x2 -> x4, starting transfers between devices: 4.2 us -> 7.12 us  [swapped(): lax.ppermute(block, axis, [(i, i + 1) for i in lower] + [(i + 1, i) for i...]
    ppermute x2 -> x4, waiting for transfers between devices: 1.92 us -> 3.55 us  [swapped(): lax.ppermute(block, axis, [(i, i + 1) for i in lower] + [(i + 1, i) for i...]
    all_to_all x1, waiting for transfers between devices: 0.01 us -> 1.12 us  [per_device(): lax.all_to_all(packed, ('lat', 'lon'), split_axis=0, concat_axis=0, tiled...]
  transfers between devices with their start and end apart: 7 -> 7, of which waited for: 2 -> 4; matrix products, arithmetic and copies ran while one was open for 0% -> 0% of each run, Pallas kernels for 27% -> 27%
where the time goes in v3:
time: 45.7 us; the launch traced here: 45.4 us
  Pallas kernels  23.4 us (51%)
  starting transfers between devices  15.3 us (33%)
  waiting for transfers between devices  5.88 us (13%)
  between operations  0.72 us (2%)
    pallas_call x1, Pallas kernels, run_steps(): pl.pallas_call(steps_body, name='three_steps', out_shape=jax.ShapeDtypeSt...  8.93 us
    ppermute x4, starting transfers between devices, swapped(): lax.ppermute(block, axis, [(i, i + 1) for i in lower] + [(i + 1, i) for i...  7.12 us
    all_to_all x1, starting transfers between devices, per_device(): lax.all_to_all(packed, ('lat', 'lon'), split_axis=0, concat_axis=0, tiled...  6.05 us
    pallas_call x1, Pallas kernels, own_strips(): pl.pallas_call(own_body, name='own_strips', out_shape=(jax.ShapeDtypeStru...  4.92 us
    pallas_call x1, Pallas kernels, outer_columns(): pl.pallas_call(columns_body, name='outer_columns', out_shape=(jax.ShapeDt...  3.67 us
    ppermute x4, waiting for transfers between devices, swapped(): lax.ppermute(block, axis, [(i, i + 1) for i in lower] + [(i + 1, i) for i...  3.55 us
    pallas_call x1, Pallas kernels, place_records(): pl.pallas_call(place_body, name='place_records', out_shape=(jax.ShapeDtyp...  2.67 us
    pallas_call x1, Pallas kernels, pack_records(): pl.pallas_call(functools.partial(pack_body, n_lon), name='pack_records',...  2.22 us
  transfers between devices with their start and end apart: 7, of which 4 were waited for; matrix products, arithmetic and copies ran while one was open for 0% of the time, Pallas kernels for 27%

profile of v3, /device:TPU:8, one launch (start us, length us, event | category | flops | bytes accessed | tf_op | source)
XLA Modules:
  0.0 45.4 jit_solution(10364251620187235669)
XLA Ops:
  0.7 2.2 %pack_records.1 = bf16[32,21,4,128]{3,2,1,0:T(4,128)(2,1)} custom-call(s32[1]{0:T(128)S(6)} %copy.10.live_ref, s32[1,64]{1,0:T(1,128)} %tile_in.1, s32[1,64]{1,0:T(1,128)} %block_in.1, bf16[1280,128]{1,0:T(8,128)(2,1)} %bitcast.7), custom_call_target="tpu_custom_call" | custom-call | tf_op jit(solution)/shard_map/pack_records/pallas_call | solution.py:124
  2.9 6.0 %all-to-all-start = ((bf16[32,21,4,128]{3,2,1,0:T(4,128)(2,1)}), bf16[32,21,4,128]{3,2,1,0:T(4,128)(2,1)S(1)}, u32[]{:S(2)}, u32[]{:S(2)}) async-start(bf16[32,21,4,128]{3,2,1,0:T(4,128)(2,1)} %pack_records.1), calls=%async_computation | async-start | bytes 1376256 | tf_op jit(solution)/shard_map/all_to_all | solution.py:780
  8.9 3.7 %outer_columns.1 = (bf16[128,384]{1,0:T(8,128)(2,1)S(1)}, bf16[10,2,128,128]{3,2,1,0:T(8,128)(2,1)S(1)}) custom-call(f32[2,10,128,256]{3,2,1,0:T(8,128)} %adj_hbm.5, f32[10,128,256]{2,1,0:T(8,128)} %ef_hbm.5, f32[10,128,256]{2,1,0:T(8,128)} %nf_hbm.5, s32[10,128,256]{2,1,0:T(8,128)} %mask_hbm.1), custom_call_target="tpu_custom_call" | custom-call | tf_op jit(solution)/shard_map/outer_columns/pallas_call | solution.py:215
  12.6 2.2 %collective-permute-start.1 = (bf16[128,384]{1,0:T(8,128)(2,1)S(1)}, bf16[128,384]{1,0:T(8,128)(2,1)S(1)}, u32[]{:S(2)}, u32[]{:S(2)}) collective-permute-start(bf16[128,384]{1,0:T(8,128)(2,1)S(1)} %get-tuple-element.23), channel_id=1, source_target_pairs={{0,7},{1,0},{2,1},{3,2},{4,3},{5,4},{6,5},{7,6},{8,15},{9,8},{10,9... | collective-permute-start | bytes 294920 | tf_op jit(solution)/shard_map/ppermute | solution.py:754
  14.8 0.0 collective-permute-start
  14.8 4.9 %own_strips.1 = (f32[3,3,128,128]{3,2,1,0:T(8,128)S(1)}, bf16[128,384]{1,0:T(8,128)(2,1)S(1)}, bf16[2,128,384]{2,1,0:T(8,128)(2,1)S(1)}, f32[9,128,256]{2,1,0:T(...) custom-call(f32[10,128,256]{2,1,0:T(8,128)} %ef_hbm.5, f32[10,128,256]{2,1,0:T(8,128)} %nf_hbm.5, ...), custom_call_target="tpu_custom_call" | custom-call | flops 100000000 | bytes 10000000 | tf_op jit(solution)/shard_map/own_strips/pallas_call | solution.py:305
  19.7 0.0 collective-permute-done.1.east
  19.7 1.2 %collective-permute-done.west = bf16[128,384]{1,0:T(8,128)(2,1)S(1)} collective-permute-done((bf16[128,384]{1,0:T(8,128)(2,1)S(1)}, bf16[128,384]{1,0:T(8,128)(2,1)S(1)}, u32[]{:S(2)}, u32[]{:S(2)}) %collective-permute-start) | collective-permute-done | bytes 98336 | tf_op jit(solution)/shard_map/ppermute | solution.py:754
  20.9 0.9 %outer_rows.1 = (f32[3,3,128,128]{3,2,1,0:T(8,128)S(1)}, bf16[3,128,128]{2,1,0:T(8,128)(2,1)S(1)}, bf16[12,16,256]{2,1,0:T(8,128)(2,1)}, bf16[12,16,256]{2,1,0:T(8,128)(2,1)}) custom-call(s32[1]{0:T(128)} %bitcast.3.odd_ref, bf16[128,384]{1,0:T(8,128)(2,1)S(1)} %collective-permute-done.west, bf16[128,384]{1,0:T(8,128)(2,1)S(1)} %collective-permute-done.1.east, ...), custom_call_target="tpu_custom_call" | custom-call | tf_op jit(solution)/shard_map/outer_rows/pallas_call | solution.py:367
  21.9 0.0 collective-permute-start.4
  21.9 4.1 %collective-permute-start.5 = (bf16[12,16,256]{2,1,0:T(8,128)(2,1)}, bf16[12,16,256]{2,1,0:T(8,128)(2,1)S(1)}, u32[]{:S(2)}, u32[]{:S(2)}) collective-permute-start(bf16[12,16,256]{2,1,0:T(8,128)(2,1)} %get-tuple-element.36), channel_id=1, source_target_pairs={{8,16},{16,8},{9,17},{17,9},{10,18},{18,10},{11,19},{19,11},{12,20... | collective-permute-start | bytes 294920 | tf_op jit(solution)/shard_map/ppermute | solution.py:760
  26.0 1.1 %all-to-all-done.arrived_ref = bf16[32,21,4,128]{3,2,1,0:T(4,128)(2,1)S(1)} async-done(((bf16[32,21,4,128]{3,2,1,0:T(4,128)(2,1)}), bf16[32,21,4,128]{3,2,1,0:T(4,128)(2,1)S(1)}, u32[]{:S(2)}, u32[]{:S(2)}) %all-to-all-start) | async-done | bytes 688160 | tf_op jit(solution)/shard_map/all_to_all | solution.py:780
  27.2 0.0 copy-start
  27.2 2.7 %place_records.1 = (f32[20,2,128,128]{3,2,1,0:T(8,128)S(1)}, f32[3,128,128]{2,1,0:T(8,128)S(1)}, bf16[11,8,256]{2,1,0:T(8,128)(2,1)S(1)}, bf16[11,8,256]{2,1,0:T(8,128)(2,1)S(1)}) custom-call(s32[1]{0:T(128)} %bitcast.3.odd_ref, bf16[32,21,4,128]{3,2,1,0:T(4,128)(2,1)S(1)} %all-to-all-done.arrived_ref, f32[9,128,256]{2,1,0:T(8,128)S(1)} %get-tuple-element.22.first_ref, ...), custom_call_target="tpu_custom_call" | custom-call | tf_op jit(solution)/shard_map/place_records/pallas_call | solution.py:481
  29.8 0.7 %collective-permute-start.2 = (bf16[11,8,256]{2,1,0:T(8,128)(2,1)S(1)}, bf16[11,8,256]{2,1,0:T(8,128)(2,1)S(1)}, u32[]{:S(2)}, u32[]{:S(2)}) collective-permute-start(bf16[11,8,256]{2,1,0:T(8,128)(2,1)S(1)} %get-tuple-element.33), channel_id=1, source_target_pairs={{0,8},{16,24},{8,0},{24,16},{1,9},{17,25},{9,1},{25,17},{2,10},{18... | collective-permute-start | bytes 135176 | tf_op jit(solution)/shard_map/ppermute | solution.py:760
  30.5 2.3 %collective-permute-start.3 = (bf16[11,8,256]{2,1,0:T(8,128)(2,1)S(1)}, bf16[11,8,256]{2,1,0:T(8,128)(2,1)S(1)}, u32[]{:S(2)}, u32[]{:S(2)}) collective-permute-start(bf16[11,8,256]{2,1,0:T(8,128)(2,1)S(1)} %get-tuple-element.34), channel_id=1, source_target_pairs={{8,16},{16,8},{9,17},{17,9},{10,18},{18,10},{11,19},{19,11},{12,20... | collective-permute-start | bytes 135176 | tf_op jit(solution)/shard_map/ppermute | solution.py:760
  32.8 0.1 add_convert_fusion.where_ref
  32.9 0.0 collective-permute-done.4.low_ref
  32.9 0.0 collective-permute-done.5.high_ref
  32.9 1.0 %collective-permute-done.2.swap_a_ref = bf16[11,8,256]{2,1,0:T(8,128)(2,1)S(1)} collective-permute-done((bf16[11,8,256]{2,1,0:T(8,128)(2,1)S(1)}, bf16[11,8,256]{2,1,0:T(8,128)(2,1)S(1)}, u32[]{:S(2)}, u32[]{:S(2)}) %collective-permute-start.2) | collective-permute-done | bytes 45088 | tf_op jit(solution)/shard_map/ppermute | solution.py:760
  34.0 2.5 %collective-permute-done.3.swap_b_ref = bf16[11,8,256]{2,1,0:T(8,128)(2,1)S(1)} collective-permute-done((bf16[11,8,256]{2,1,0:T(8,128)(2,1)S(1)}, bf16[11,8,256]{2,1,0:T(8,128)(2,1)S(1)}, u32[]{:S(2)}, u32[]{:S(2)}) %collective-permute-start.3) | collective-permute-done | bytes 45088 | tf_op jit(solution)/shard_map/ppermute | solution.py:760
  36.4 0.0 copy-done
  36.4 8.9 %three_steps.1 = f32[2,10,128,256]{3,2,1,0:T(8,128)} custom-call(s32[3]{0:T(128)S(1)} %add_convert_fusion.where_ref, f32[2,10]{1,0:T(2,128)S(1)} %copy-done, f32[20,2,128,128]{3,2,1,0:T(8,128)S(1)} %get-tuple-element.31.state_ref, f32[3,128,128]{2,1,0:T(8,128)S(1)} %get-tuple-element.32.strip_ref, bf16[11,8,256]{2,1,0:T(8,128)(2,1)S(1)} %collective-permute-done.2.swap_a_ref, ...), custom_call_target="tpu_custom_call" | custom-call | tf_op jit(solution)/shard_map/three_steps/pallas_call | solution.py:724
Async XLA Ops:
  2.9 24.3 %all-to-all-start = ((bf16[32,21,4,128]{3,2,1,0:T(4,128)(2,1)}), bf16[32,21,4,128]{3,2,1,0:T(4,128)(2,1)S(1)}, u32[]{:S(2)}, u32[]{:S(2)}) async-start(bf16[32,21,4,128]{3,2,1,0:T(4,128)(2,1)} %pack_records.1), calls=%async_computation | async-start | bytes 1376256 | tf_op jit(solution)/shard_map/all_to_all | solution.py:780
  12.6 7.1 %collective-permute-start.1 = (bf16[128,384]{1,0:T(8,128)(2,1)S(1)}, bf16[128,384]{1,0:T(8,128)(2,1)S(1)}, u32[]{:S(2)}, u32[]{:S(2)}) collective-permute-start(bf16[128,384]{1,0:T(8,128)(2,1)S(1)} %get-tuple-element.23), channel_id=1, source_target_pairs={{0,7},{1,0},{2,1},{3,2},{4,3},{5,4},{6,5},{7,6},{8,15},{9,8},{10,9... | collective-permute-start | bytes 294920 | tf_op jit(solution)/shard_map/ppermute | solution.py:754
  14.8 6.1 %collective-permute-start = (bf16[128,384]{1,0:T(8,128)(2,1)S(1)}, bf16[128,384]{1,0:T(8,128)(2,1)S(1)}, u32[]{:S(2)}, u32[]{:S(2)}) collective-permute-start(bf16[128,384]{1,0:T(8,128)(2,1)S(1)} %get-tuple-element.23), channel_id=1, source_target_pairs={{0,1},{1,2},{2,3},{3,4},{4,5},{5,6},{6,7},{7,0},{8,9},{9,10},{10,1... | collective-permute-start | bytes 294920 | tf_op jit(solution)/shard_map/ppermute | solution.py:754
  21.9 11.0 %collective-permute-start.4 = (bf16[12,16,256]{2,1,0:T(8,128)(2,1)}, bf16[12,16,256]{2,1,0:T(8,128)(2,1)S(1)}, u32[]{:S(2)}, u32[]{:S(2)}) collective-permute-start(bf16[12,16,256]{2,1,0:T(8,128)(2,1)} %get-tuple-element.35), channel_id=1, source_target_pairs={{0,8},{16,24},{8,0},{24,16},{1,9},{17,25},{9,1},{25,17},{2,10},{18... | collective-permute-start | bytes 294920 | tf_op jit(solution)/shard_map/ppermute | solution.py:760
  21.9 11.0 %collective-permute-start.5 = (bf16[12,16,256]{2,1,0:T(8,128)(2,1)}, bf16[12,16,256]{2,1,0:T(8,128)(2,1)S(1)}, u32[]{:S(2)}, u32[]{:S(2)}) collective-permute-start(bf16[12,16,256]{2,1,0:T(8,128)(2,1)} %get-tuple-element.36), channel_id=1, source_target_pairs={{8,16},{16,8},{9,17},{17,9},{10,18},{18,10},{11,19},{19,11},{12,20... | collective-permute-start | bytes 294920 | tf_op jit(solution)/shard_map/ppermute | solution.py:760
  27.2 9.3 %copy-start = (f32[2,10]{1,0:T(2,128)S(1)}, f32[2,10]{1,0:T(2,128)}, u32[]{:S(2)}) copy-start(f32[2,10]{1,0:T(2,128)} %spread_ref.1) | copy-start | bytes 244
  29.8 4.1 %collective-permute-start.2 = (bf16[11,8,256]{2,1,0:T(8,128)(2,1)S(1)}, bf16[11,8,256]{2,1,0:T(8,128)(2,1)S(1)}, u32[]{:S(2)}, u32[]{:S(2)}) collective-permute-start(bf16[11,8,256]{2,1,0:T(8,128)(2,1)S(1)} %get-tuple-element.33), channel_id=1, source_target_pairs={{0,8},{16,24},{8,0},{24,16},{1,9},{17,25},{9,1},{25,17},{2,10},{18... | collective-permute-start | bytes 135176 | tf_op jit(solution)/shard_map/ppermute | solution.py:760
  30.5 5.9 %collective-permute-start.3 = (bf16[11,8,256]{2,1,0:T(8,128)(2,1)S(1)}, bf16[11,8,256]{2,1,0:T(8,128)(2,1)S(1)}, u32[]{:S(2)}, u32[]{:S(2)}) collective-permute-start(bf16[11,8,256]{2,1,0:T(8,128)(2,1)S(1)} %get-tuple-element.34), channel_id=1, source_target_pairs={{8,16},{16,8},{9,17},{17,9},{10,18},{18,10},{11,19},{19,11},{12,20... | collective-permute-start | bytes 135176 | tf_op jit(solution)/shard_map/ppermute | solution.py:760
